TPU v7x, 32 devices: a whole 2x2x4 slice. The times are simulated.
32 devices in a mesh: dp: 8 (over z, x), mp: 4 (over y, core).
Axes of the slice: x: 2, y: 2, z: 4, core: 2. Of those that a mesh axis runs over, the one named last changes fastest.
Arguments:
- tokens: bfloat16 [256, 48, 3584], P('dp', None, 'mp'), may hold values from -180 to 180
- norm_gain: float32 [3584], replicated, may hold values from 0.1 to 1.9
- w_query: bfloat16 [3584, 3584], P('dp', 'mp'), may hold values from -0.16 to 0.16
- w_keyval: bfloat16 [3584, 2, 512], P('dp', None, 'mp'), may hold values from -0.16 to 0.16
- w_out: bfloat16 [3584, 3584], P('mp', 'dp'), may hold values from -0.09375 to 0.09375
- residents: bfloat16 [8, 2048, 3584], P('dp', 'mp'), may hold values from -6 to 6
- lengths: int32 [256], P('dp'), may hold values from 6 to 48
- cluster: int32 [256, 1], P('dp'), may hold values from 0 to 7; in each aligned block of 32 rows (0 to 31, 32 to 63, ...) at most 4 rows name the same one
- owner: int32 [8], replicated, may hold values from 0 to 7, each once
- counts: int32 [8], replicated, may hold values from 256 to 2048
- flags: int32 [256], P('dp'), may hold values 0 or 1
Outputs:
- similarity: float32 [256, 2048], P('dp', 'mp')
Inputs may be any that keep to these rules, and one draw needn't show every extreme that they name: Each dialogue's cluster; among the 32 dialogues of one index of dp (aligned blocks of rows) no cluster is named more than 4 times. owner gives every cluster a distinct index of dp that holds its residents.
All inputs are finite; a program needn't handle non-finite values. No bound on the sum of `flags` on one device may be relied on, other than what follows from the above.
Results may differ from a plain program's by a relative error of at most 0.013.
Values may be sent and summed in bfloat16 or wider, within the bound.
A program may use at most 128 MiB of HBM per device.

v0:
```python
import math

import jax
import jax.numpy as jnp
from jax import lax
from jax.sharding import PartitionSpec as P

HEAD_DIM = 128


rope_base = 1000000.0
logit_scale = 100.0


def rotate(values, positions):
    half = values.shape[-1] // 2
    freqs = rope_base ** (-jnp.arange(half, dtype=jnp.float32) * 2.0 / values.shape[-1])
    angles = positions.astype(jnp.float32)[:, None] * freqs[None, :]
    cosine = jnp.cos(angles)[:, None, :]
    sine = jnp.sin(angles)[:, None, :]
    first = values[..., :half]
    second = values[..., half:]
    return jnp.concatenate(
        [first * cosine - second * sine, second * cosine + first * sine], axis=-1
    )


def attend(query, keys, values, length):
    seq_len = query.shape[0]
    kv_count = keys.shape[1]
    group = query.shape[1] // kv_count
    grouped = query.reshape(seq_len, kv_count, group, query.shape[-1])
    scores = jnp.einsum(
        "qkgd,pkd->kgqp", grouped, keys, preferred_element_type=jnp.float32
    ) / math.sqrt(query.shape[-1])
    row_pos = jnp.arange(seq_len)[:, None]
    col_pos = jnp.arange(seq_len)[None, :]
    allowed = (col_pos <= row_pos) & (col_pos < length)
    scores = jnp.where(allowed, scores, -1e30)
    highest = jnp.max(scores, axis=-1, keepdims=True)
    expanded = jnp.exp(scores - highest)
    weights = (expanded / jnp.sum(expanded, axis=-1, keepdims=True)).astype(jnp.bfloat16)
    context = jnp.einsum("kgqp,pkd->qkgd", weights, values, preferred_element_type=jnp.float32)
    valid = (jnp.arange(seq_len) < length).astype(jnp.float32)
    pooled = jnp.sum(context * valid[:, None, None, None], axis=0) / length.astype(jnp.float32)
    return pooled.reshape(-1)


def local(
    tokens, norm_gain, w_query, w_keyval, w_out, residents, lengths, cluster, owner, counts, flags
):
    gathered = lax.all_gather(tokens, "mp", axis=2, tiled=True)
    dialogs, seq_len, width = gathered.shape
    hidden = gathered.astype(jnp.float32)
    normed = (
        hidden * lax.rsqrt(jnp.mean(hidden * hidden, axis=-1, keepdims=True) + 1e-06) * norm_gain
    ).astype(jnp.bfloat16)
    normed_flat = normed.reshape(dialogs * seq_len, width)
    query_cols = w_query.shape[1]
    keyval_cols = w_keyval.shape[2]
    pieces = (
        lax.all_gather(w_query, "dp", axis=0, tiled=True),
        lax.all_gather(w_keyval, "dp", axis=0, tiled=True),
    )
    keyval_piece = pieces[1].reshape(pieces[1].shape[0], 2 * keyval_cols)
    query_sum = jnp.dot(normed_flat, pieces[0], preferred_element_type=jnp.float32)
    keyval_sum = jnp.dot(normed_flat, keyval_piece, preferred_element_type=jnp.float32)
    positions = jnp.arange(seq_len)
    local_heads = query_cols // HEAD_DIM
    local_kv = keyval_cols // HEAD_DIM
    query = jax.vmap(lambda block: rotate(block, positions))(
        query_sum.reshape(dialogs, seq_len, local_heads, HEAD_DIM)
    ).astype(jnp.bfloat16)
    keys = jax.vmap(lambda block: rotate(block, positions))(
        keyval_sum[:, :keyval_cols].reshape(dialogs, seq_len, local_kv, HEAD_DIM)
    ).astype(jnp.bfloat16)
    values = (
        keyval_sum[:, keyval_cols:]
        .reshape(dialogs, seq_len, local_kv, HEAD_DIM)
        .astype(jnp.bfloat16)
    )
    pooled_context = jax.vmap(attend)(query, keys, values, lengths).astype(jnp.bfloat16)
    valid = (positions[None, :] < lengths[:, None]).astype(jnp.float32)
    pooled_input = (
        jnp.sum(hidden * valid[:, :, None], axis=1) / lengths.astype(jnp.float32)[:, None]
    )
    partial_out = jnp.dot(
        pooled_context,
        lax.all_gather(w_out, "dp", axis=1, tiled=True),
        preferred_element_type=jnp.float32,
    )
    projected = lax.psum(partial_out.astype(jnp.bfloat16), "mp").astype(jnp.float32)
    embedding = pooled_input + projected
    unit = embedding * lax.rsqrt(jnp.sum(embedding * embedding, axis=-1, keepdims=True) + 1e-06)
    unit = (unit * flags.astype(jnp.float32)[:, None]).astype(jnp.bfloat16)
    my_index = lax.axis_index("dp")
    owner_count = lax.axis_size("dp")
    my_count = jnp.sum(jnp.where(owner == my_index, counts, 0))
    members = residents[0]
    member_count = members.shape[0]
    inverse_norm = lax.rsqrt(
        jnp.einsum("md,md->m", members, members, preferred_element_type=jnp.float32) + 1e-06
    )
    member_start = lax.axis_index("mp") * member_count
    live = member_start + jnp.arange(member_count) < my_count
    table_size = owner.shape[0]
    cluster_ids = cluster[:, 0]
    destination = jnp.sum(
        jnp.where(jnp.arange(table_size)[None, :] == cluster_ids[:, None], owner[None, :], 0),
        axis=1,
    )
    capacity = max(1, -(-dialogs // owner_count))
    order = jnp.arange(dialogs)
    earlier = (destination[None, :] == destination[:, None]) & (order[None, :] < order[:, None])
    rank = jnp.sum(earlier.astype(jnp.int32), axis=1)
    onehot = (jnp.arange(owner_count)[:, None, None] == destination[None, None, :]) & (
        jnp.arange(capacity)[None, :, None] == rank[None, None, :]
    )
    outgoing = jnp.einsum(
        "ocn,nd->ocd", onehot.astype(jnp.bfloat16), unit, preferred_element_type=jnp.float32
    ).astype(jnp.bfloat16)
    query_rows = lax.all_to_all(outgoing, "dp", split_axis=0, concat_axis=0, tiled=True)
    dots = lax.dot_general(
        query_rows,
        members,
        (((query_rows.ndim - 1,), (1,)), ((), ())),
        preferred_element_type=jnp.float32,
    )
    returned = lax.all_to_all(
        jnp.where(live, logit_scale * dots * inverse_norm, 0.0).astype(jnp.bfloat16),
        "dp",
        split_axis=0,
        concat_axis=0,
        tiled=True,
    ).astype(jnp.float32)
    similarity = jnp.einsum(
        "ocn,ocm->nm", onehot.astype(jnp.float32), returned, precision=lax.Precision.HIGHEST
    )
    return similarity


def solution(mesh):
    in_specs = (
        P("dp", None, "mp"),
        P(),
        P("dp", "mp"),
        P("dp", None, "mp"),
        P("mp", "dp"),
        P("dp", "mp", None),
        P("dp"),
        P("dp", None),
        P(),
        P(),
        P("dp"),
    )
    out_specs = P("dp", "mp")
    return jax.shard_map(local, mesh=mesh, in_specs=in_specs, out_specs=out_specs, check_vma=False)
```

profile of v0, /device:TPU:0, one launch (start us, length us, event | category | flops | bytes accessed | tf_op | source)
XLA Modules:
  0.0 408.5 jit_solution(2310838354348667568)
XLA Ops:
  6.5 0.7 all-gather.9.cloned.1.call-update
  7.3 0.7 all-gather.5.cloned.1.call-update
  8.1 0.7 all-gather.7.cloned.1.call-update
  9.4 0.7 convert_element_type.91
  10.0 0.7 convert_element_type.99
  10.7 0.8 select_reduce_fusion
  11.7 0.7 iota_compare_fusion.1
  12.9 2.8 fusion.6
  15.7 97.3 %all-gather.9.cloned.1.call-done = bf16[3584,896]{1,0:T(8,128)(2,1)} async-done(((bf16[448,896]{1,0:T(8,128)(2,1)}), bf16[3584,896]{1,0:T(8,128)(2,1)}) %all-gather.9.cloned.1.call-update) | async-done | bytes 6422544 | tf_op jit(solution)/shard_map/all_gather | solution.py:62
  113.0 9.7 %copy.20 = bf16[896,3584]{1,0:T(8,128)(2,1)} copy(bf16[896,3584]{0,1:T(8,128)(2,1)} %bitcast.86) | data formatting | bytes 12845056 | tf_op jit(solution)/shard_map/dot_general | solution.py:66
  122.7 63.2 %all-gather.5.cloned.1.call-done = bf16[32,48,3584]{2,1,0:T(8,128)(2,1)} async-done(((bf16[32,48,896]{2,1,0:T(8,128)(2,1)}), bf16[32,48,3584]{2,1,0:T(8,128)(2,1)}) %all-gather.5.cloned.1.call-update) | async-done | bytes 11010064 | tf_op jit(solution)/shard_map/all_gather | solution.py:52
  185.8 8.9 %fusion = (f32[32,3584]{1,0:T(8,128)S(1)}, f32[32,48]{1,0:T(8,128)S(1)}) fusion(bf16[32,48,3584]{2,1,0:T(8,128)(2,1)} %all-gather.5.cloned.1.call-done, f32[32,48]{1,0:T(8,128)S(1)} %get-tuple-element.14), kind=kLoop, calls=%fused_computation.3 | loop fusion | flops 27408896 | bytes 11481088 | tf_op jit(solution)/shard_map/reduce_sum | solution.py:85
  194.8 11.0 %fusion.3 = bf16[32,48,3584]{2,1,0:T(8,128)(2,1)} fusion(bf16[32,48,3584]{2,1,0:T(8,128)(2,1)} %all-gather.5.cloned.1.call-done, f32[3584]{0:T(1024)S(1)} %copy-done.1, f32[32,48]{1,0:T(8,128)S(1)} %add_rsqrt_fusion), kind=kLoop, calls=%fused_computation.6 | loop fusion | flops 22020096 | bytes 22040576 | tf_op jit(solution)/shard_map/convert_element_type | solution.py:57
  205.7 28.8 %all-gather.7.cloned.1.call-done = bf16[3584,2,128]{2,1,0:T(2,128)(2,1)} async-done(((bf16[448,2,128]{2,1,0:T(2,128)(2,1)}), bf16[3584,2,128]{2,1,0:T(2,128)(2,1)}) %all-gather.7.cloned.1.call-update) | async-done | bytes 1835024 | tf_op jit(solution)/shard_map/all_gather | solution.py:63
  234.5 7.2 %fusion.22 = f32[1536,256]{1,0:T(8,128)S(1)} fusion(bf16[1536,3584]{1,0:T(8,128)(2,1)} %bitcast.84, bf16[448,8,2,128]{3,2,1,0:T(2,128)(2,1)} %bitcast.92), kind=kOutput, calls=%fused_computation.34 | convolution fusion | flops 2818572288 | bytes 14417920 | tf_op jit(solution)/shard_map/dot_general | solution.py:67
  242.4 1.5 slice-done.1
  243.8 11.6 %fusion.4 = f32[32,48,7,128]{3,1,2,0:T(8,128)S(1)} fusion(bf16[7,128,3584,1]{2,1,0,3:T(8,128)(2,1)S(1)} %bitcast.89, bf16[32,48,3584]{2,1,0:T(8,128)(2,1)S(1)} %copy-done), kind=kOutput, calls=%fused_computation.7 | convolution fusion | flops 9865003008 | bytes 22937600 | tf_op jit(solution)/shard_map/dot_general | solution.py:66
  255.5 1.9 subtract_convert_fusion
  257.4 3.6 fusion.9
  261.0 2.1 fusion.8
  263.2 2.3 fusion.7
  265.5 70.8 %all-gather.11.cloned.1.call-done = bf16[896,3584]{0,1:T(8,128)(2,1)} async-done(((bf16[896,448]{0,1:T(8,128)(2,1)}), bf16[896,3584]{0,1:T(8,128)(2,1)}) %all-gather.11.cloned.1.call-update) | async-done | bytes 6422544 | tf_op jit(solution)/shard_map/all_gather | solution.py:89
  336.3 5.5 %convolution_convert_fusion.1 = bf16[32,3584]{1,0:T(8,128)(2,1)} fusion(bf16[896,3584]{0,1:T(8,128)(2,1)} %all-gather.11.cloned.1.call-done, f32[4,8,7,128]{3,2,1,0:T(8,128)S(1)} %bitcast.91, f32[32]{0:T(128)S(1)} %convert_element_type.91), kind=kOutput, calls=%fused_computation.20 | convolution fusion | flops 205692928 | bytes 6766720 | tf_op jit(solution)/shard_map/dot_general | solution.py:87
  341.8 30.2 %all-reduce.2.cloned.1.call-done = bf16[32,3584]{1,0:T(8,128)(2,1)} async-done(((bf16[32,3584]{1,0:T(8,128)(2,1)}), bf16[32,3584]{1,0:T(8,128)(2,1)}) %all-reduce.2.cloned.1.call-update) | async-done | bytes 229392 | tf_op jit(solution)/shard_map/psum | solution.py:92
  372.0 1.2 multiply_reduce_fusion
  373.2 1.9 convolution_convert_fusion
  375.1 5.5 %all-to-all-start = ((bf16[8,4,3584]{2,1,0:T(4,128)(2,1)}), bf16[8,4,3584]{2,1,0:T(4,128)(2,1)S(1)}, u32[]{:S(2)}, u32[]{:S(2)}) async-start(bf16[8,4,3584]{2,1,0:T(4,128)(2,1)} %convolution_convert_fusion), calls=%async_computation | async-start | bytes 458752 | tf_op jit(solution)/shard_map/all_to_all | solution.py:122
  381.3 0.7 add_compare_fusion
  382.0 6.7 %all-to-all-done = bf16[8,4,3584]{2,1,0:T(4,128)(2,1)S(1)} async-done(((bf16[8,4,3584]{2,1,0:T(4,128)(2,1)}), bf16[8,4,3584]{2,1,0:T(4,128)(2,1)S(1)}, u32[]{:S(2)}, u32[]{:S(2)}) %all-to-all-start) | async-done | bytes 229408 | tf_op jit(solution)/shard_map/all_to_all | solution.py:122
  388.7 3.2 fusion.33
  391.9 9.2 %all_to_all.10 = bf16[8,4,512]{2,1,0:T(4,128)(2,1)S(1)} all-to-all(bf16[8,4,512]{2,1,0:T(4,128)(2,1)S(1)} %fusion.33), channel_id=1, replica_groups=mesh['dp'=8,'mp'=4] {'dp'}, dimensions={0} | all-to-all | bytes 65536 | tf_op jit(solution)/shard_map/all_to_all | solution.py:129
  401.2 0.8 convolution_bitcast_fusion
  (35 shorter events, 2.7 us)
Async XLA Ops:
  6.5 106.4 %all-gather.9.cloned.1.call-start = ((), (), s32[]{:S(2)}) async-start(), calls=%async_computation.4 | async-start | bytes 7225344 | tf_op jit(solution)/shard_map/all_gather | solution.py:62
  7.3 178.6 %all-gather.5.cloned.1.call-start = ((), (), s32[]{:S(2)}) async-start(), calls=%async_computation.2 | async-start | bytes 13762560 | tf_op jit(solution)/shard_map/all_gather | solution.py:52
  8.0 226.5 %all-gather.7.cloned.1.call-start = ((), (), s32[]{:S(2)}) async-start(), calls=%async_computation.3 | async-start | bytes 2064384 | tf_op jit(solution)/shard_map/all_gather | solution.py:63
  8.7 327.5 %all-gather.11.cloned.1.call-start = ((), (), s32[]{:S(2)}) async-start(), calls=%async_computation.5 | async-start | bytes 7225344 | tf_op jit(solution)/shard_map/all_gather | solution.py:89
  9.3 362.7 %all-reduce.2.cloned.1.call-start = ((), (), s32[]{:S(2)}) async-start(), calls=%async_computation.6 | async-start | bytes 458752 | tf_op jit(solution)/shard_map/psum | solution.py:92
  185.8 8.9 %copy-start.1 = (f32[3584]{0:T(1024)S(1)}, f32[3584]{0:T(1024)}, u32[]{:S(2)}) copy-start(f32[3584]{0:T(1024)} %param.12) | copy-start | bytes 43012
  194.8 47.4 %slice-start = ((s8[6422528]{0:T(1024)(128)(4,1)}), s8[2228224]{0:T(1024)(128)(4,1)S(1)}, s32[]{:S(2)}) async-start(s8[6422528]{0:T(1024)(128)(4,1)} %bitcast.87), calls=%async_computation.7 | async-start | bytes 4456448
  234.5 7.8 %copy-start = (bf16[32,48,3584]{2,1,0:T(8,128)(2,1)S(1)}, bf16[32,48,3584]{2,1,0:T(8,128)(2,1)}, u32[]{:S(2)}) copy-start(bf16[32,48,3584]{2,1,0:T(8,128)(2,1)} %fusion.3) | copy-start | bytes 33030148
  234.5 9.3 %slice-start.1 = ((s8[6422528]{0:T(1024)(128)(4,1)}), s8[4194304]{0:T(1024)(128)(4,1)S(1)}, s32[]{:S(2)}) async-start(s8[6422528]{0:T(1024)(128)(4,1)} %bitcast.87), calls=%async_computation.8 | async-start | bytes 8388608
  265.5 115.2 %copy-start.2 = (s32[8]{0:T(128)S(1)}, s32[8]{0:T(128)}, u32[]{:S(2)}) copy-start(s32[8]{0:T(128)} %param.19) | copy-start | bytes 100
  265.5 115.2 %copy-start.3 = (s32[8]{0:T(128)S(1)}, s32[8]{0:T(128)}, u32[]{:S(2)}) copy-start(s32[8]{0:T(128)} %param.20) | copy-start | bytes 100
  375.1 13.5 %all-to-all-start = ((bf16[8,4,3584]{2,1,0:T(4,128)(2,1)}), bf16[8,4,3584]{2,1,0:T(4,128)(2,1)S(1)}, u32[]{:S(2)}, u32[]{:S(2)}) async-start(bf16[8,4,3584]{2,1,0:T(4,128)(2,1)} %convolution_convert_fusion), calls=%async_computation | async-start | bytes 458752 | tf_op jit(solution)/shard_map/all_to_all | solution.py:122
Sparse Core Ops, SparseCore 0:
  9.5 103.3 all-gather.8
  114.5 71.2 all-gather.4
  188.0 46.4 all-gather.6
  236.6 99.6 all-gather.10
  341.9 30.0 all-reduce.1
where the time goes:
time: 409 us
  waiting for transfers between devices  299 us (73%)
  matrix products  36.3 us (9%)
  other arithmetic  33 us (8%)
  between operations  13.3 us (3%)
  local copies, waits for them, and re-layouts  11.5 us (3%)
  blocking collectives  9.24 us (2%)
  starting transfers between devices  5.66 us (1%)
    all_gather x1, waiting for transfers between devices, local(): lax.all_gather(w_query, 'dp', axis=0, tiled=True)  97.3 us
    all_gather x1, waiting for transfers between devices, local(): lax.all_gather(w_out, 'dp', axis=1, tiled=True)  70.8 us
    all_gather x1, waiting for transfers between devices, local(): gathered = lax.all_gather(tokens, 'mp', axis=2, tiled=True)  63.2 us
    psum x1, waiting for transfers between devices, local(): lax.psum(partial_out.astype(jnp.bfloat16), 'mp').astype(jnp.float32)  30.2 us
    all_gather x1, waiting for transfers between devices, local(): lax.all_gather(w_keyval, 'dp', axis=0, tiled=True)  28.8 us
    dot_general x1, matrix products, local(): jnp.dot(normed_flat, pieces[0], preferred_element_type=jnp.float32)  11.6 us
    convert_element_type x1, other arithmetic, local(): normed = (hidden * lax.rsqrt(jnp.mean(hidden * hidden, axis=-1, keepdims=...  11 us
    dot_general x1, local copies, waits for them, and re-layouts, local(): jnp.dot(normed_flat, pieces[0], preferred_element_type=jnp.float32)  9.72 us
  transfers between devices with their start and end apart: 6, of which 6 were waited for; matrix products, arithmetic and copies ran while one was open for 16% of the time, Pallas kernels for 0%

commit v1 on v0

--- a/solution.py
+++ b/solution.py
@@ -3,6 +3,8 @@
 import jax
 import jax.numpy as jnp
 from jax import lax
+from jax.experimental import pallas as pl
+from jax.experimental.pallas import tpu as pltpu
 from jax.sharding import PartitionSpec as P
 
 HEAD_DIM = 128
@@ -46,9 +48,244 @@
     return pooled.reshape(-1)
 
 
-def local(
-    tokens, norm_gain, w_query, w_keyval, w_out, residents, lengths, cluster, owner, counts, flags
+MESH = pl.DeviceIdType.MESH
+ROWS = 384
+
+
+def gather_project_kernel(
+    tin, win, gain, mask, cosine, sine, qkv, pooled,
+    tok, wbuf, scaled, acc, squares,
+    tsend, trecv, wsend, wrecv, lsem,
 ):
+    dp = lax.axis_index("dp")
+    mp = lax.axis_index("mp")
+    z, x = dp // 2, dp % 2
+    core_peer = mp + 1 - 2 * (mp % 2)
+    y_peer = (mp + 2) % 4
+    far = (core_peer + 2) % 4
+    x_peer = 2 * z + 1 - x
+    total = tin.shape[0]
+
+    barrier = pltpu.get_barrier_semaphore()
+
+    def greet(dp_to, mp_to):
+        pl.semaphore_signal(
+            barrier, inc=1, device_id={"dp": dp_to, "mp": mp_to}, device_id_type=MESH
+        )
+
+    greet(dp, core_peer)
+    greet(dp, y_peer)
+    greet(x_peer, mp)
+    has_up, has_down = z < 3, z > 0
+
+    @pl.when(has_up)
+    def _():
+        greet(dp + 2, mp)
+
+    @pl.when(has_down)
+    def _():
+        greet(dp - 2, mp)
+
+    @pl.when(has_up & has_down)
+    def _():
+        pl.semaphore_wait(barrier, 5)
+
+    @pl.when(jnp.logical_not(has_up & has_down))
+    def _():
+        pl.semaphore_wait(barrier, 4)
+
+    def token_copy(index, source, slot, mp_to):
+        return pltpu.make_async_remote_copy(
+            src_ref=source, dst_ref=tok.at[slot], send_sem=tsend.at[index],
+            recv_sem=trecv.at[index], device_id={"dp": dp, "mp": mp_to}, device_id_type=MESH,
+        )
+
+    def weight_copy(way, z_from, source):
+        slot = 2 * z_from + x
+        dp_to = (dp + 2, dp - 2, x_peer)[way]
+        return pltpu.make_async_remote_copy(
+            src_ref=wbuf.at[slot] if source is None else source, dst_ref=wbuf.at[slot],
+            send_sem=wsend.at[way, z_from], recv_sem=wrecv.at[slot],
+            device_id={"dp": dp_to, "mp": mp}, device_id_type=MESH,
+        )
+
+    def weight_arrival(slot):
+        pltpu.make_async_remote_copy(
+            src_ref=wbuf.at[slot], dst_ref=wbuf.at[slot], send_sem=wsend.at[0, 0],
+            recv_sem=wrecv.at[slot], device_id={"dp": x_peer, "mp": mp}, device_id_type=MESH,
+        ).wait_recv()
+
+    across = token_copy(0, tin, mp, y_peer)
+    across.start()
+
+    @pl.when(has_up)
+    def _():
+        weight_copy(0, z, win).start()
+
+    @pl.when(has_down)
+    def _():
+        weight_copy(1, z, win).start()
+
+    weight_copy(2, z, win).start()
+    beside = token_copy(1, tin, mp, core_peer)
+    beside.start()
+    own = pltpu.make_async_copy(win, wbuf.at[dp], lsem)
+    own.start()
+
+    squares[...] = jnp.zeros_like(squares)
+
+    def prepare(source, slot):
+        @pl.loop(0, total // 96)
+        def _(step):
+            rows = pl.ds(pl.multiple_of(step * 96, 96), 96)
+            values = source[rows, :].astype(jnp.float32)
+            squares[rows, :] += jnp.sum(values * values, axis=-1, keepdims=True)
+            scaled[slot, rows, :] = (values * gain[slot]).astype(jnp.bfloat16)
+
+        pooled[slot] = jnp.dot(mask[...], source[...], preferred_element_type=jnp.float32)
+
+    prepare(tin, mp)
+    beside.wait_recv()
+    prepare(tok.at[core_peer], core_peer)
+    own.wait()
+
+    def relay(k):
+        @pl.when(z >= k)
+        def _():
+            weight_arrival(2 * (z - k) + x)
+
+            @pl.when(has_up)
+            def _():
+                weight_copy(0, z - k, None).start()
+
+            weight_copy(2, z - k, None).start()
+
+        @pl.when(z + k <= 3)
+        def _():
+            weight_arrival(2 * (z + k) + x)
+
+            @pl.when(has_down)
+            def _():
+                weight_copy(1, z + k, None).start()
+
+            weight_copy(2, z + k, None).start()
+
+    relay(1)
+    relay(2)
+    across.wait_recv()
+    onward = token_copy(2, tok.at[y_peer], y_peer, core_peer)
+    onward.start()
+    relay(3)
+    prepare(tok.at[y_peer], y_peer)
+    onward.wait_recv()
+    prepare(tok.at[far], far)
+
+    width = 4 * tin.shape[1]
+    columns = win.shape[1]
+
+    def multiply(turn):
+        block = (z, z + 1 - 2 * (z % 2), (z + 2) % 4, 3 - z)[turn]
+        weight_arrival(2 * block + 1 - x)
+        weights = wbuf.at[pl.ds(2 * block, 2)]
+
+        @pl.loop(0, total // ROWS)
+        def _(step):
+            rows = pl.ds(pl.multiple_of(step * ROWS, ROWS), ROWS)
+            product = jnp.dot(
+                scaled[block, rows, :],
+                weights[...].reshape(2 * win.shape[0], columns),
+                preferred_element_type=jnp.float32,
+            )
+            if turn == 0:
+                acc[rows, :] = product
+            else:
+                acc[rows, :] += product
+
+    for turn in range(4):
+        multiply(turn)
+
+    @pl.loop(0, total // ROWS)
+    def _(step):
+        rows = pl.ds(pl.multiple_of(step * ROWS, ROWS), ROWS)
+        scale = lax.rsqrt(squares[rows, :] * (1.0 / width) + 1e-06)
+        for head in range(columns // HEAD_DIM):
+            span = pl.ds(head * HEAD_DIM, HEAD_DIM)
+            piece = acc[rows, span] * scale
+            if head < columns // HEAD_DIM - 1:
+                piece = piece * cosine[...] + pltpu.roll(piece, HEAD_DIM // 2, 1) * sine[...]
+            qkv[rows, span] = piece.astype(jnp.bfloat16)
+
+    across.wait_send()
+    beside.wait_send()
+    onward.wait_send()
+
+    for z_from in range(4):
+        @pl.when(has_up & (z >= z_from))
+        def _():
+            weight_copy(0, z_from, None).wait_send()
+
+        @pl.when(has_down & (z <= z_from))
+        def _():
+            weight_copy(1, z_from, None).wait_send()
+
+        weight_copy(2, z_from, None).wait_send()
+
+
+def gather_project(tokens, norm_gain, w_query, w_keyval, lengths):
+    dialogs, seq_len, part = tokens.shape
+    total = dialogs * seq_len
+    weights = jnp.concatenate([w_query, w_keyval.reshape(w_keyval.shape[0], -1)], axis=1)
+    depth, columns = weights.shape
+    positions = jnp.arange(seq_len)
+    half = HEAD_DIM // 2
+    freqs = rope_base ** (-jnp.arange(half, dtype=jnp.float32) * 2.0 / HEAD_DIM)
+    angles = positions.astype(jnp.float32)[:, None] * freqs[None, :]
+    cosine = jnp.cos(angles)
+    sine = jnp.sin(angles)
+    cosine = jnp.tile(jnp.concatenate([cosine, cosine], axis=1), (ROWS // seq_len, 1))
+    sine = jnp.tile(jnp.concatenate([-sine, sine], axis=1), (ROWS // seq_len, 1))
+    row = jnp.arange(total)[None, :]
+    mine = jnp.arange(dialogs)[:, None]
+    mask = ((row // seq_len == mine) & (row % seq_len < lengths[:, None])).astype(jnp.bfloat16)
+    vmem = pl.BlockSpec(memory_space=pltpu.VMEM)
+    qkv, pooled = pl.pallas_call(
+        gather_project_kernel,
+        out_shape=(
+            jax.ShapeDtypeStruct((total, columns), jnp.bfloat16),
+            jax.ShapeDtypeStruct((4, dialogs, part), jnp.float32),
+        ),
+        in_specs=[vmem] * 6,
+        out_specs=(vmem, vmem),
+        scratch_shapes=[
+            pltpu.VMEM((4, total, part), jnp.bfloat16),
+            pltpu.VMEM((8, depth, columns), jnp.bfloat16),
+            pltpu.VMEM((4, total, part), jnp.bfloat16),
+            pltpu.VMEM((total, columns), jnp.float32),
+            pltpu.VMEM((total, 1), jnp.float32),
+            pltpu.SemaphoreType.DMA((3,)),
+            pltpu.SemaphoreType.DMA((3,)),
+            pltpu.SemaphoreType.DMA((3, 4)),
+            pltpu.SemaphoreType.DMA((8,)),
+            pltpu.SemaphoreType.DMA,
+        ],
+        compiler_params=pltpu.CompilerParams(
+            collective_id=0, has_side_effects=True, vmem_limit_bytes=58 * 1024 * 1024
+        ),
+    )(
+        tokens.reshape(total, part), weights, norm_gain.reshape(4, 1, part), mask, cosine, sine
+    )
+    pooled_input = (pooled / lengths.astype(jnp.float32)[None, :, None]).transpose(1, 0, 2)
+    queries = w_query.shape[1]
+    shape = (dialogs, seq_len, -1, HEAD_DIM)
+    return (
+        qkv[:, :queries].reshape(shape),
+        qkv[:, queries : queries + HEAD_DIM].reshape(shape),
+        qkv[:, queries + HEAD_DIM :].reshape(shape),
+        pooled_input.reshape(dialogs, 4 * part),
+    )
+
+
+def plain_project(tokens, norm_gain, w_query, w_keyval, lengths):
     gathered = lax.all_gather(tokens, "mp", axis=2, tiled=True)
     dialogs, seq_len, width = gathered.shape
     hidden = gathered.astype(jnp.float32)
@@ -79,17 +316,29 @@
         .reshape(dialogs, seq_len, local_kv, HEAD_DIM)
         .astype(jnp.bfloat16)
     )
-    pooled_context = jax.vmap(attend)(query, keys, values, lengths).astype(jnp.bfloat16)
     valid = (positions[None, :] < lengths[:, None]).astype(jnp.float32)
     pooled_input = (
         jnp.sum(hidden * valid[:, :, None], axis=1) / lengths.astype(jnp.float32)[:, None]
     )
-    partial_out = jnp.dot(
-        pooled_context,
-        lax.all_gather(w_out, "dp", axis=1, tiled=True),
-        preferred_element_type=jnp.float32,
-    )
-    projected = lax.psum(partial_out.astype(jnp.bfloat16), "mp").astype(jnp.float32)
+    return query, keys, values, pooled_input
+
+
+def local(
+    tokens, norm_gain, w_query, w_keyval, w_out, residents, lengths, cluster, owner, counts, flags
+):
+    if lax.axis_size("dp") == 8 and lax.axis_size("mp") == 4:
+        project = gather_project
+    else:
+        project = plain_project
+    query, keys, values, pooled_input = project(tokens, norm_gain, w_query, w_keyval, lengths)
+    dialogs = query.shape[0]
+    pooled_context = jax.vmap(attend)(query, keys, values, lengths).astype(jnp.bfloat16)
+    everyone = lax.all_gather(pooled_context, "dp", axis=0, tiled=True)
+    slices = jnp.dot(everyone, w_out, preferred_element_type=jnp.float32).astype(jnp.bfloat16)
+    slices = slices.reshape(-1, dialogs, w_out.shape[1])
+    slices = lax.all_to_all(slices, "dp", split_axis=0, concat_axis=0, tiled=True)
+    partial_out = slices.transpose(1, 0, 2).reshape(dialogs, -1)
+    projected = lax.psum(partial_out, "mp").astype(jnp.float32)
     embedding = pooled_input + projected
     unit = embedding * lax.rsqrt(jnp.sum(embedding * embedding, axis=-1, keepdims=True) + 1e-06)
     unit = (unit * flags.astype(jnp.float32)[:, None]).astype(jnp.bfloat16)

time: 409 us -> 256 us (0.63)
  waiting for transfers between devices: 299 us -> 41.8 us
  Pallas kernels: 0 us -> 107 us
  blocking collectives: 9.24 us -> 41.8 us
  matrix products: 36.3 us -> 13.7 us
  other arithmetic: 33 us -> 14.4 us
    all_gather x4 -> x0, waiting for transfers between devices: 260 us -> none  [the longest x1 97.3 us: local(): lax.all_gather(w_query, 'dp', axis=0, tiled=True)]
    pallas_call x0 -> x1, Pallas kernels: none -> 107 us  [gather_project(): pl.pallas_call(gather_project_kernel, out_shape=(jax.ShapeDtypeStruct((to...]
    all_gather x0 -> x1, blocking collectives: none -> 32.5 us  [local(): everyone = lax.all_gather(pooled_context, 'dp', axis=0, tiled=True)]
    dot_general x3 -> x1, matrix products: 24.3 us -> 0.44 us  [local(): jnp.dot(everyone, w_out, preferred_element_type=jnp.float32)]
    dot_general x1 -> x0, local copies, waits for them, and re-layouts: 9.72 us -> none  [local(): jnp.dot(normed_flat, pieces[0], preferred_element_type=jnp.float32)]
    convert_element_type x3 -> x4, other arithmetic: 11.6 us -> 1.99 us  [the longest x1 1.4 us: gather_project(): ((row // seq_len == mine) & (row % seq_len < lengths[:, None])).astype(jn...]
    reduce_sum x1 -> x0, other arithmetic: 8.89 us -> none  [local(): jnp.sum(hidden * valid[:, :, None], axis=1)]
    another operation x0 -> x3, local copies, waits for them, and re-layouts: none -> 5.52 us
  transfers between devices with their start and end apart: 6 -> 3, of which waited for: 6 -> 3; matrix products, arithmetic and copies ran while one was open for 16% -> 2% of each run, Pallas kernels for 0% -> 0%
where the time goes in v1:
time: 256 us; the launch traced here: 255 us
  Pallas kernels  107 us (42%)
  blocking collectives  41.8 us (16%)
  waiting for transfers between devices  41.8 us (16%)
  other arithmetic  14.4 us (6%)
  local copies, waits for them, and re-layouts  14 us (5%)
  matrix products  13.7 us (5%)
  between operations  13.7 us (5%)
  starting transfers between devices  8.96 us (4%)
    pallas_call x1, Pallas kernels, gather_project(): pl.pallas_call(gather_project_kernel, out_shape=(jax.ShapeDtypeStruct((to...  107 us
    all_gather x1, blocking collectives, local(): everyone = lax.all_gather(pooled_context, 'dp', axis=0, tiled=True)  32.5 us
    psum x1, waiting for transfers between devices, local(): projected = lax.psum(partial_out, 'mp').astype(jnp.float32)  30.3 us
    all_to_all x1, blocking collectives, local(): lax.all_to_all(jnp.where(live, logit_scale * dots * inverse_norm, 0.0).as...  9.24 us
    all_to_all x1, waiting for transfers between devices, local(): lax.all_to_all(outgoing, 'dp', split_axis=0, concat_axis=0, tiled=True)  6.7 us
    all_to_all x1, starting transfers between devices, local(): lax.all_to_all(outgoing, 'dp', split_axis=0, concat_axis=0, tiled=True)  5.51 us
  transfers between devices with their start and end apart: 3, of which 3 were waited for; matrix products, arithmetic and copies ran while one was open for 2% of the time, Pallas kernels for 0%

profile of v1, /device:TPU:0, one launch (start us, length us, event | category | flops | bytes accessed | tf_op | source)
XLA Modules:
  0.0 255.2 jit_solution(16991792528195158909)
XLA Ops:
  6.6 1.0 copy.53
  7.6 1.3 reshape.227.gain
  9.1 2.2 pad_maximum_fusion.win
  11.4 1.4 fusion.30.mask
  12.8 0.7 tile.8
  13.5 0.7 tile.20
  14.2 106.8 %shard_map.109 = (bf16[1536,1152]{1,0:T(8,128)(2,1)}, f32[4,32,896]{2,1,0:T(8,128)}) custom-call(bf16[1536,896]{1,0:T(8,128)(2,1)} %bitcast.77, bf16[448,1152]{1,0:T(8,128)(2,1)} %pad_maximum_fusion.win, f32[4,1,896]{2,1,0:T(1,128)} %reshape.227.gain, bf16[32,1536]{1,0:T(8,128)(2,1)} %fusion.30.mask, f32[384,128]{1,0:T(8,128)} %bitcast.81, f32[384,128]{1,0:T(8,128)} %bitcast.82), custom_call_target="tpu_custom_call" | custom-call | tf_op jit(solution)/shard_map/pallas_call | solution.py:251
  121.0 2.1 fusion.47
  123.1 2.0 slice.11
  125.1 0.7 iota_compare_fusion.2
  125.8 0.6 iota_compare_fusion.1
  126.9 4.1 %reshape.231 = bf16[32,48,7,128]{3,2,1,0:T(8,128)(2,1)} reshape(bf16[1536,896]{1,0:T(8,128)(2,1)S(1)} %slice.11) | data formatting | bytes 5505024 | tf_op jit(solution)/shard_map/reshape.18
  131.0 1.0 broadcast_and_fusion
  132.0 5.0 %fusion.3 = (f32[32,7,48]{2,1,0:T(8,128)S(1)}, f32[32,48,48,7]{2,1,3,0:T(8,128)S(1)}) fusion(pred[32,48,48]{1,2,0:T(8,128)(4,1)S(1)} %broadcast_and_fusion, bf16[32,48,128,1]{2,1,3,0:T(8,128)(2,1)} %bitcast.78, bf16[32,48,7,128]{3,2,1,0:T(8,128)(2,1)} %reshape.231), kind=kOutput, calls=%fused_computation.9 | convolution fusion | flops 133658112 | bytes 5326848 | tf_op jit(solution)/shard_map/vmap(qkgd,pkd->kgqp)/dot_general | solution.py:35
  137.0 2.1 fusion.2
  139.2 2.3 fusion.1
  141.6 32.5 %all_gather.3 = bf16[256,896]{1,0:T(8,128)(2,1)S(1)} all-gather(bf16[32,896]{1,0:T(8,128)(2,1)S(1)} %fusion.31), channel_id=1, replica_groups=mesh['dp'=8,'mp'=4] {'dp'}, dimensions={0}, use_global_device_ids=true | all-gather | bytes 516096 | tf_op jit(solution)/shard_map/all_gather | solution.py:336
  174.6 0.8 copy.29
  175.4 3.4 %all-to-all-start = ((bf16[8,32,448]{2,1,0:T(8,128)(2,1)}), bf16[8,32,448]{2,1,0:T(8,128)(2,1)S(1)}, u32[]{:S(2)}, u32[]{:S(2)}) async-start(bf16[8,32,448]{2,1,0:T(8,128)(2,1)} %bitcast.16), calls=%async_computation | async-start | bytes 524288 | tf_op jit(solution)/shard_map/all_to_all | solution.py:339
  179.4 2.8 %fusion = f32[512]{0:T(512)S(1)} fusion(bf16[1,512,3584]{2,1,0:T(8,128)(2,1)} %param.16), kind=kLoop, calls=%fused_computation.1 | loop fusion | flops 5504512 | bytes 3672064 | tf_op jit(solution)/shard_map/md,md->m/dot_general | solution.py:351
  182.2 4.8 %all-to-all-done = bf16[8,32,448]{2,1,0:T(8,128)(2,1)S(1)} async-done(((bf16[8,32,448]{2,1,0:T(8,128)(2,1)}), bf16[8,32,448]{2,1,0:T(8,128)(2,1)S(1)}, u32[]{:S(2)}, u32[]{:S(2)}) %all-to-all-start) | async-done | bytes 229408 | tf_op jit(solution)/shard_map/all_to_all | solution.py:339
  187.1 1.0 reshape.234
  188.1 30.3 %all-reduce.2.cloned.1.call-done = bf16[32,3584]{1,0:T(8,128)(2,1)} async-done(((bf16[32,3584]{1,0:T(8,128)(2,1)}), bf16[32,3584]{1,0:T(8,128)(2,1)}) %all-reduce.2.cloned.1.call-update) | async-done | bytes 229392 | tf_op jit(solution)/shard_map/psum | solution.py:341
  218.5 1.1 multiply_reduce_fusion
  219.6 1.9 convolution_convert_fusion
  221.5 5.5 %all-to-all-start.1 = ((bf16[8,4,3584]{2,1,0:T(4,128)(2,1)}), bf16[8,4,3584]{2,1,0:T(4,128)(2,1)S(1)}, u32[]{:S(2)}, u32[]{:S(2)}) async-start(bf16[8,4,3584]{2,1,0:T(4,128)(2,1)} %convolution_convert_fusion), calls=%async_computation.1 | async-start | bytes 458752 | tf_op jit(solution)/shard_map/all_to_all | solution.py:371
  227.0 0.6 fusion.43
  227.6 0.7 add_compare_fusion
  228.3 6.7 %all-to-all-done.1 = bf16[8,4,3584]{2,1,0:T(4,128)(2,1)S(1)} async-done(((bf16[8,4,3584]{2,1,0:T(4,128)(2,1)}), bf16[8,4,3584]{2,1,0:T(4,128)(2,1)S(1)}, u32[]{:S(2)}, u32[]{:S(2)}) %all-to-all-start.1) | async-done | bytes 229408 | tf_op jit(solution)/shard_map/all_to_all | solution.py:371
  235.0 3.2 %fusion.22 = bf16[8,4,512]{2,1,0:T(4,128)(2,1)S(1)} fusion(bf16[8,4,3584]{2,1,0:T(4,128)(2,1)S(1)} %all-to-all-done.1, bf16[1,512,3584]{2,1,0:T(8,128)(2,1)} %param.16, f32[512]{0:T(512)S(1)} %rsqrt_multiply_fusion, pred[512]{0:T(512)(128)(4,1)S(1)} %add_compare_fusion), kind=kOutput, calls=%fused_computation.24 | convolution fusion | flops 117489664 | bytes 3934720 | tf_op jit(solution)/shard_map/dot_general | solution.py:372
  238.3 9.2 %all_to_all.15 = bf16[8,4,512]{2,1,0:T(4,128)(2,1)S(1)} all-to-all(bf16[8,4,512]{2,1,0:T(4,128)(2,1)S(1)} %fusion.22), channel_id=1, replica_groups=mesh['dp'=8,'mp'=4] {'dp'}, dimensions={0} | all-to-all | bytes 65536 | tf_op jit(solution)/shard_map/all_to_all | solution.py:378
  247.5 0.8 convolution_bitcast_fusion
  (41 shorter events, 2.0 us)
Async XLA Ops:
  6.5 167.6 %copy-start = (bf16[896,448]{0,1:T(8,128)(2,1)S(1)}, bf16[896,448]{0,1:T(8,128)(2,1)}, u32[]{:S(2)}) copy-start(bf16[896,448]{0,1:T(8,128)(2,1)} %param.15) | copy-start | bytes 2408452
  14.2 110.9 %copy-start.5 = (s32[32]{0:T(128)S(1)}, s32[32]{0:T(128)}, u32[]{:S(2)}) copy-start(s32[32]{0:T(128)} %param.17) | copy-start | bytes 388
  132.0 7.1 %copy-start.2 = (bf16[1536,128]{1,0:T(8,128)(2,1)S(1)}, bf16[1536,128]{1,0:T(8,128)(2,1)}, u32[]{:S(2)}) copy-start(bf16[1536,128]{1,0:T(8,128)(2,1)} %get-tuple-element.10) | copy-start | bytes 1179652
  132.0 7.1 %copy-start.3 = (f32[32,48]{1,0:T(8,128)S(1)}, f32[32,48]{1,0:T(8,128)}, u32[]{:S(2)}) copy-start(f32[32,48]{1,0:T(8,128)} %get-tuple-element.15) | copy-start | bytes 18436
  139.1 2.4 copy-start.4
  139.2 39.7 %copy-start.6 = (s32[8]{0:T(128)S(1)}, s32[8]{0:T(128)}, u32[]{:S(2)}) copy-start(s32[8]{0:T(128)} %param.19) | copy-start | bytes 100
  139.2 39.7 %copy-start.8 = (s32[32,1]{0,1:T(1,128)S(1)}, s32[32,1]{0,1:T(1,128)}, u32[]{:S(2)}) copy-start(s32[32,1]{0,1:T(1,128)} %param.18) | copy-start | bytes 388
  139.2 40.0 %copy-start.1 = (f32[4,32,896]{2,1,0:T(8,128)S(1)}, f32[4,32,896]{2,1,0:T(8,128)}, u32[]{:S(2)}) copy-start(f32[4,32,896]{2,1,0:T(8,128)} %get-tuple-element.7) | copy-start | bytes 1376260
  139.2 40.1 %copy-start.9 = (s32[32]{0:T(128)S(1)}, s32[32]{0:T(128)}, u32[]{:S(2)}) copy-start(s32[32]{0:T(128)} %param.21) | copy-start | bytes 388
  174.1 52.9 %copy-start.7 = (s32[8]{0:T(128)S(1)}, s32[8]{0:T(128)}, u32[]{:S(2)}) copy-start(s32[8]{0:T(128)} %param.20) | copy-start | bytes 100
  175.4 11.6 %all-to-all-start = ((bf16[8,32,448]{2,1,0:T(8,128)(2,1)}), bf16[8,32,448]{2,1,0:T(8,128)(2,1)S(1)}, u32[]{:S(2)}, u32[]{:S(2)}) async-start(bf16[8,32,448]{2,1,0:T(8,128)(2,1)} %bitcast.16), calls=%async_computation | async-start | bytes 524288 | tf_op jit(solution)/shard_map/all_to_all | solution.py:339
  178.8 39.6 %all-reduce.2.cloned.1.call-start = ((), (), s32[]{:S(2)}) async-start(), calls=%async_computation.3 | async-start | bytes 458752 | tf_op jit(solution)/shard_map/psum | solution.py:341
  221.5 13.5 %all-to-all-start.1 = ((bf16[8,4,3584]{2,1,0:T(4,128)(2,1)}), bf16[8,4,3584]{2,1,0:T(4,128)(2,1)S(1)}, u32[]{:S(2)}, u32[]{:S(2)}) async-start(bf16[8,4,3584]{2,1,0:T(4,128)(2,1)} %convolution_convert_fusion), calls=%async_computation.1 | async-start | bytes 458752 | tf_op jit(solution)/shard_map/all_to_all | solution.py:371
Sparse Core Ops, SparseCore 0:
  188.3 30.1 all-reduce.1

commit v2 on v1

--- a/solution.py
+++ b/solution.py
@@ -285,6 +285,207 @@
     )
 
 
+def score_kernel(
+    context, pooled, onehot, w_out, members, live, returned,
+    own_rows, own_pooled, all_rows, all_pooled, exact, parts, others, sums, rows_in, joined,
+    squares, replies, arrived,
+    a_send, a_recv, c_send, c_recv, d_send, d_recv, f_send, f_recv,
+):
+    dp = lax.axis_index("dp")
+    mp = lax.axis_index("mp")
+    barrier = pltpu.get_barrier_semaphore()
+    for i in range(8):
+        for j in range(4):
+            if i or j:
+                pl.semaphore_signal(
+                    barrier, inc=1, device_id={"dp": (dp + i) % 8, "mp": (mp + j) % 4},
+                    device_id_type=MESH,
+                )
+
+    for o in range(8):
+        own_pooled[o] = jnp.dot(
+            onehot[...], pooled[o], preferred_element_type=jnp.float32
+        ).astype(jnp.bfloat16)
+    own_rows[...] = jnp.dot(
+        onehot[...], context[...], preferred_element_type=jnp.float32
+    ).astype(jnp.bfloat16)
+    pl.semaphore_wait(barrier, 31)
+
+    def remote(source, target, send, recv, dp_to, mp_to):
+        return pltpu.make_async_remote_copy(
+            src_ref=source, dst_ref=target, send_sem=send, recv_sem=recv,
+            device_id={"dp": dp_to, "mp": mp_to}, device_id_type=MESH,
+        )
+
+    def rows_copy(i, slot):
+        return remote(
+            own_rows, all_rows.at[slot], a_send.at[0, i], a_recv.at[0, slot], (dp + i) % 8, mp
+        )
+
+    def pooled_copy(i, slot):
+        to = (dp + i) % 8
+        return remote(
+            own_pooled.at[to], all_pooled.at[slot], a_send.at[1, i], a_recv.at[1, slot], to, mp
+        )
+
+    for i in range(1, 8):
+        rows_copy(i, dp).start()
+    for i in range(1, 8):
+        pooled_copy(i, dp).start()
+    all_rows[dp] = own_rows[...]
+    all_pooled[dp] = own_pooled[dp]
+
+    @pl.loop(0, members.shape[0] // 64)
+    def _(step):
+        rows = pl.ds(pl.multiple_of(step * 64, 64), 64)
+        values = members[rows, :].astype(jnp.float32)
+        squares[rows, :] = jnp.broadcast_to(
+            jnp.sum(values * values, axis=-1, keepdims=True), (64, 128)
+        )
+
+    scale = live[...] * lax.rsqrt(squares[...].T[0:1, :] + 1e-06)
+    row = lax.broadcasted_iota(jnp.int32, (256, 256), 0)
+    column = lax.broadcasted_iota(jnp.int32, (256, 256), 1)
+    target = ((row >> 2) & 7) * 32 + (row >> 5) * 4 + (row & 3)
+    order = jnp.where(column == target, 1.0, 0.0).astype(jnp.bfloat16)
+    for i in range(1, 8):
+        rows_copy(i, (dp + i) % 8).wait_recv()
+    sorted_rows = jnp.dot(
+        order, all_rows[...].reshape(256, -1), preferred_element_type=jnp.float32
+    ).astype(jnp.bfloat16)
+    product = jnp.dot(sorted_rows, w_out[...], preferred_element_type=jnp.float32)
+    parts[...] = product.astype(jnp.bfloat16).reshape(parts.shape)
+
+    def part_copy(i, slot):
+        to = (mp + i) % 4
+        return remote(parts.at[to], others.at[slot], c_send.at[i], c_recv.at[slot], dp, to)
+
+    for i in range(1, 4):
+        part_copy(i, mp).start()
+    for i in range(1, 8):
+        pooled_copy(i, (dp + i) % 8).wait_recv()
+    exact[...] = (
+        product
+        + jnp.dot(order, all_pooled[...].reshape(256, -1), preferred_element_type=jnp.float32)
+    ).reshape(exact.shape)
+    total = exact[mp]
+    for i in range(1, 4):
+        slot = (mp + i) % 4
+        part_copy(i, slot).wait_recv()
+        total = total + others[slot].astype(jnp.float32)
+    sums[...] = total.astype(jnp.bfloat16).reshape(sums.shape)
+
+    def sum_copy(j, i, slot):
+        return remote(
+            sums.at[j], rows_in.at[slot], d_send.at[j, i], d_recv.at[slot],
+            2 * mp + j, (mp + i) % 4,
+        )
+
+    for j in range(2):
+        mine = 2 * mp + j == dp
+
+        @pl.when(jnp.logical_not(mine))
+        def _():
+            sum_copy(j, 0, dp).start()
+
+        for i in range(1, 4):
+            sum_copy(j, i, dp).start()
+
+        @pl.when(mine)
+        def _():
+            rows_in[dp] = sums[j]
+
+    for slot in range(8):
+        @pl.when(jnp.logical_not((dp // 2 == mp) & (dp == slot)))
+        def _():
+            sum_copy(0, 0, slot).wait_recv()
+
+    width = rows_in.shape[2]
+    for slot in range(8):
+        joined[:, slot * width : (slot + 1) * width] = rows_in[slot].astype(jnp.float32)
+    embedding = joined[...]
+    unit = embedding * lax.rsqrt(jnp.sum(embedding * embedding, axis=-1, keepdims=True) + 1e-06)
+    dots = lax.dot_general(
+        unit.astype(jnp.bfloat16), members[...], (((1,), (1,)), ((), ())),
+        preferred_element_type=jnp.float32,
+    )
+    found = (dots * scale).astype(jnp.bfloat16)
+    row = lax.broadcasted_iota(jnp.int32, (128, 32), 0)
+    column = lax.broadcasted_iota(jnp.int32, (128, 32), 1)
+    spread = jnp.where(((row & 15) < 4) & (column == (row >> 4) * 4 + (row & 15)), 1.0, 0.0)
+    replies[...] = jnp.dot(
+        spread.astype(jnp.bfloat16), found, preferred_element_type=jnp.float32
+    ).astype(jnp.bfloat16).reshape(replies.shape)
+
+    def reply_copy(i, slot):
+        to = (dp + i) % 8
+        return remote(replies.at[to], arrived.at[slot], f_send.at[i], f_recv.at[slot], to, mp)
+
+    for i in range(1, 8):
+        reply_copy(i, dp).start()
+    arrived[dp] = replies[dp]
+    for i in range(1, 8):
+        reply_copy(i, (dp + i) % 8).wait_recv()
+    returned[...] = arrived[...]
+
+    for i in range(1, 8):
+        rows_copy(i, dp).wait_send()
+        pooled_copy(i, dp).wait_send()
+        reply_copy(i, dp).wait_send()
+    for i in range(1, 4):
+        part_copy(i, mp).wait_send()
+    for j in range(2):
+        @pl.when(2 * mp + j != dp)
+        def _():
+            sum_copy(j, 0, dp).wait_send()
+
+        for i in range(1, 4):
+            sum_copy(j, i, dp).wait_send()
+
+
+def score(pooled_context, pooled_input, w_out, members, onehot, live):
+    dialogs, head_width = pooled_context.shape
+    width = w_out.shape[1]
+    member_count = members.shape[0]
+    slots = onehot.reshape(-1, dialogs).astype(jnp.bfloat16)
+    pooled = pooled_input.astype(jnp.bfloat16).reshape(dialogs, 8, width).transpose(1, 0, 2)
+    vmem = pl.BlockSpec(memory_space=pltpu.VMEM)
+    half, full = jnp.bfloat16, jnp.float32
+    returned = pl.pallas_call(
+        score_kernel,
+        out_shape=jax.ShapeDtypeStruct((8, 16, member_count), half),
+        in_specs=[vmem] * 6,
+        out_specs=vmem,
+        scratch_shapes=[
+            pltpu.VMEM((32, head_width), half),
+            pltpu.VMEM((8, 32, width), half),
+            pltpu.VMEM((8, 32, head_width), half),
+            pltpu.VMEM((8, 32, width), half),
+            pltpu.VMEM((4, 64, width), full),
+            pltpu.VMEM((4, 64, width), half),
+            pltpu.VMEM((4, 64, width), half),
+            pltpu.VMEM((2, 32, width), half),
+            pltpu.VMEM((8, 32, width), half),
+            pltpu.VMEM((32, 8 * width), full),
+            pltpu.VMEM((member_count, 128), full),
+            pltpu.VMEM((8, 16, member_count), half),
+            pltpu.VMEM((8, 16, member_count), half),
+            pltpu.SemaphoreType.DMA((2, 8)),
+            pltpu.SemaphoreType.DMA((2, 8)),
+            pltpu.SemaphoreType.DMA((4,)),
+            pltpu.SemaphoreType.DMA((4,)),
+            pltpu.SemaphoreType.DMA((2, 4)),
+            pltpu.SemaphoreType.DMA((8,)),
+            pltpu.SemaphoreType.DMA((8,)),
+            pltpu.SemaphoreType.DMA((8,)),
+        ],
+        compiler_params=pltpu.CompilerParams(
+            collective_id=1, has_side_effects=True, vmem_limit_bytes=32 * 1024 * 1024
+        ),
+    )(pooled_context, pooled, slots, w_out, members, live)
+    return returned[:, : onehot.shape[1]]
+
+
 def plain_project(tokens, norm_gain, w_query, w_keyval, lengths):
     gathered = lax.all_gather(tokens, "mp", axis=2, tiled=True)
     dialogs, seq_len, width = gathered.shape
@@ -323,16 +524,8 @@
     return query, keys, values, pooled_input
 
 
-def local(
-    tokens, norm_gain, w_query, w_keyval, w_out, residents, lengths, cluster, owner, counts, flags
-):
-    if lax.axis_size("dp") == 8 and lax.axis_size("mp") == 4:
-        project = gather_project
-    else:
-        project = plain_project
-    query, keys, values, pooled_input = project(tokens, norm_gain, w_query, w_keyval, lengths)
-    dialogs = query.shape[0]
-    pooled_context = jax.vmap(attend)(query, keys, values, lengths).astype(jnp.bfloat16)
+def plain_score(pooled_context, pooled_input, w_out, members, onehot, live):
+    dialogs = pooled_context.shape[0]
     everyone = lax.all_gather(pooled_context, "dp", axis=0, tiled=True)
     slices = jnp.dot(everyone, w_out, preferred_element_type=jnp.float32).astype(jnp.bfloat16)
     slices = slices.reshape(-1, dialogs, w_out.shape[1])
@@ -341,29 +534,9 @@
     projected = lax.psum(partial_out, "mp").astype(jnp.float32)
     embedding = pooled_input + projected
     unit = embedding * lax.rsqrt(jnp.sum(embedding * embedding, axis=-1, keepdims=True) + 1e-06)
-    unit = (unit * flags.astype(jnp.float32)[:, None]).astype(jnp.bfloat16)
-    my_index = lax.axis_index("dp")
-    owner_count = lax.axis_size("dp")
-    my_count = jnp.sum(jnp.where(owner == my_index, counts, 0))
-    members = residents[0]
-    member_count = members.shape[0]
+    unit = unit.astype(jnp.bfloat16)
     inverse_norm = lax.rsqrt(
         jnp.einsum("md,md->m", members, members, preferred_element_type=jnp.float32) + 1e-06
-    )
-    member_start = lax.axis_index("mp") * member_count
-    live = member_start + jnp.arange(member_count) < my_count
-    table_size = owner.shape[0]
-    cluster_ids = cluster[:, 0]
-    destination = jnp.sum(
-        jnp.where(jnp.arange(table_size)[None, :] == cluster_ids[:, None], owner[None, :], 0),
-        axis=1,
-    )
-    capacity = max(1, -(-dialogs // owner_count))
-    order = jnp.arange(dialogs)
-    earlier = (destination[None, :] == destination[:, None]) & (order[None, :] < order[:, None])
-    rank = jnp.sum(earlier.astype(jnp.int32), axis=1)
-    onehot = (jnp.arange(owner_count)[:, None, None] == destination[None, None, :]) & (
-        jnp.arange(capacity)[None, :, None] == rank[None, None, :]
     )
     outgoing = jnp.einsum(
         "ocn,nd->ocd", onehot.astype(jnp.bfloat16), unit, preferred_element_type=jnp.float32
@@ -375,17 +548,55 @@
         (((query_rows.ndim - 1,), (1,)), ((), ())),
         preferred_element_type=jnp.float32,
     )
-    returned = lax.all_to_all(
-        jnp.where(live, logit_scale * dots * inverse_norm, 0.0).astype(jnp.bfloat16),
+    return lax.all_to_all(
+        jnp.where(live[0] > 0, live[0] * dots * inverse_norm, 0.0).astype(jnp.bfloat16),
         "dp",
         split_axis=0,
         concat_axis=0,
         tiled=True,
-    ).astype(jnp.float32)
+    )
+
+
+def local(
+    tokens, norm_gain, w_query, w_keyval, w_out, residents, lengths, cluster, owner, counts, flags
+):
+    fast = lax.axis_size("dp") == 8 and lax.axis_size("mp") == 4
+    if fast:
+        project = gather_project
+    else:
+        project = plain_project
+    query, keys, values, pooled_input = project(tokens, norm_gain, w_query, w_keyval, lengths)
+    dialogs = query.shape[0]
+    pooled_context = jax.vmap(attend)(query, keys, values, lengths).astype(jnp.bfloat16)
+    my_index = lax.axis_index("dp")
+    owner_count = lax.axis_size("dp")
+    my_count = jnp.sum(jnp.where(owner == my_index, counts, 0))
+    members = residents[0]
+    member_count = members.shape[0]
+    member_start = lax.axis_index("mp") * member_count
+    live = jnp.where(member_start + jnp.arange(member_count) < my_count, logit_scale, 0.0)[None, :]
+    table_size = owner.shape[0]
+    cluster_ids = cluster[:, 0]
+    destination = jnp.sum(
+        jnp.where(jnp.arange(table_size)[None, :] == cluster_ids[:, None], owner[None, :], 0),
+        axis=1,
+    )
+    capacity = max(1, -(-dialogs // owner_count))
+    order = jnp.arange(dialogs)
+    earlier = (destination[None, :] == destination[:, None]) & (order[None, :] < order[:, None])
+    rank = jnp.sum(earlier.astype(jnp.int32), axis=1)
+    onehot = (jnp.arange(owner_count)[:, None, None] == destination[None, None, :]) & (
+        jnp.arange(capacity)[None, :, None] == rank[None, None, :]
+    )
+    if fast:
+        assign = score
+    else:
+        assign = plain_score
+    returned = assign(pooled_context, pooled_input, w_out, members, onehot, live)
     similarity = jnp.einsum(
-        "ocn,ocm->nm", onehot.astype(jnp.float32), returned, precision=lax.Precision.HIGHEST
-    )
-    return similarity
+        "ocn,ocm->nm", onehot.astype(jnp.bfloat16), returned, preferred_element_type=jnp.float32
+    )
+    return similarity * flags.astype(jnp.float32)[:, None]
 
 
 def solution(mesh):

time: 256 us -> 183 us (0.71)
  Pallas kernels: 107 us -> 149 us
  blocking collectives: 41.8 us -> 0 us
  waiting for transfers between devices: 41.8 us -> 0 us
  between operations: 13.7 us -> 0.3 us
  starting transfers between devices: 8.96 us -> 0 us
  matrix products: 13.7 us -> 7.09 us
  other arithmetic: 14.4 us -> 8.73 us
  local copies, waits for them, and re-layouts: 14 us -> 17.9 us
    pallas_call x0 -> x1, Pallas kernels: none -> 42.2 us  [score(): pl.pallas_call(score_kernel, out_shape=jax.ShapeDtypeStruct((8, 16, membe...]
    all_gather x1 -> x0, blocking collectives: 32.5 us -> none  [local(): everyone = lax.all_gather(pooled_context, 'dp', axis=0, tiled=True)]
    psum x1 -> x0, waiting for transfers between devices: 30.3 us -> none  [local(): projected = lax.psum(partial_out, 'mp').astype(jnp.float32)]
    all_to_all x2 -> x0, waiting for transfers between devices: 11.5 us -> none  [the longest x1 6.7 us: local(): lax.all_to_all(outgoing, 'dp', split_axis=0, concat_axis=0, tiled=True)]
    all_to_all x1 -> x0, blocking collectives: 9.24 us -> none  [local(): lax.all_to_all(jnp.where(live, logit_scale * dots * inverse_norm, 0.0).as...]
    all_to_all x2 -> x0, starting transfers between devices: 8.92 us -> none  [the longest x1 5.51 us: local(): lax.all_to_all(outgoing, 'dp', split_axis=0, concat_axis=0, tiled=True)]
    dot_general x4 -> x1, matrix products: 6.42 us -> 0.82 us  [local(): jnp.einsum('ocn,ocm->nm', onehot.astype(jnp.bfloat16), returned, preferre...]
    dot_general x1 -> x0, other arithmetic: 2.83 us -> none  [local(): jnp.einsum('md,md->m', members, members, preferred_element_type=jnp.float32)]
  transfers between devices with their start and end apart: 3 -> 0, of which waited for: 3 -> 0; matrix products, arithmetic and copies ran while one was open for 2% -> 0% of each run, Pallas kernels for 0% -> 0%
where the time goes in v2:
time: 183 us
  Pallas kernels  149 us (81%)
  local copies, waits for them, and re-layouts  17.9 us (10%)
  other arithmetic  8.73 us (5%)
  matrix products  7.09 us (4%)
    pallas_call x1, Pallas kernels, gather_project(): pl.pallas_call(gather_project_kernel, out_shape=(jax.ShapeDtypeStruct((to...  107 us
    pallas_call x1, Pallas kernels, score(): pl.pallas_call(score_kernel, out_shape=jax.ShapeDtypeStruct((8, 16, membe...  42.2 us
    another operation x1, local copies, waits for them, and re-layouts  5.37 us
    dot_general x1, matrix products, attend(): jnp.einsum('qkgd,pkd->kgqp', grouped, keys, preferred_element_type=jnp.fl...  3.98 us
    unnamed x20, local copies, waits for them, and re-layouts  3.8 us

profile of v2, /device:TPU:0, one launch (start us, length us, event | category | flops | bytes accessed | tf_op | source)
XLA Modules:
  0.0 183.0 jit_solution(9084168841109904764)
XLA Ops:
  0.0 0.7 iota_compare_fusion.2
  0.7 1.0 copy.46
  1.7 2.2 %pad_maximum_fusion.win = bf16[448,1152]{1,0:T(8,128)(2,1)} fusion(bf16[448,256]{1,0:T(8,128)(2,1)S(1)} %bitcast.66, bf16[448,896]{1,0:T(8,128)(2,1)} %param.13), kind=kLoop, calls=%fused_computation.17 | loop fusion | flops 2064384 | bytes 2064384 | tf_op jit(solution)/shard_map/concatenate | solution.py:237
  3.9 1.3 reshape.234.gain
  5.2 1.4 fusion.16.mask
  6.7 0.2 fusion.30
  6.8 0.1 pad_maximum_fusion.1
  6.9 0.7 tile.8
  7.6 0.7 tile.20
  8.3 106.8 %shard_map.109 = (bf16[1536,1152]{1,0:T(8,128)(2,1)}, f32[4,32,896]{2,1,0:T(8,128)}) custom-call(bf16[1536,896]{1,0:T(8,128)(2,1)} %bitcast.64, bf16[448,1152]{1,0:T(8,128)(2,1)} %pad_maximum_fusion.win, f32[4,1,896]{2,1,0:T(1,128)} %reshape.234.gain, bf16[32,1536]{1,0:T(8,128)(2,1)} %fusion.16.mask, f32[384,128]{1,0:T(8,128)} %bitcast.67, f32[384,128]{1,0:T(8,128)} %bitcast.68), custom_call_target="tpu_custom_call" | custom-call | tf_op jit(solution)/shard_map/pallas_call | solution.py:251
  115.1 2.1 %fusion.35 = (bf16[1536,128]{1,0:T(8,128)(2,1)}, bf16[1536,128]{1,0:T(8,128)(2,1)}) fusion(bf16[1536,1152]{1,0:T(8,128)(2,1)} %get-tuple-element.7), kind=kLoop, calls=%fused_computation.66 | loop fusion | bytes 1572864 | tf_op jit(solution)/shard_map/slice | solution.py:282
  117.2 0.3 broadcast_and_fusion
  117.4 3.6 %slice.14 = bf16[1536,896]{1,0:T(8,128)(2,1)} slice(bf16[1536,1152]{1,0:T(8,128)(2,1)} %get-tuple-element.7), slice={[0:1536], [0:896]} | slice | bytes 5505024 | tf_op jit(solution)/shard_map/slice | solution.py:281
  121.0 5.4 %reshape.237 = bf16[32,48,7,128]{3,2,1,0:T(8,128)(2,1)S(1)} reshape(bf16[1536,896]{1,0:T(8,128)(2,1)} %slice.14) | data formatting | bytes 5505024 | tf_op jit(solution)/shard_map/reshape.18
  126.4 4.0 %fusion.2 = (f32[32,7,48]{2,1,0:T(8,128)S(1)}, f32[32,48,48,7]{2,1,3,0:T(8,128)S(1)}) fusion(pred[32,48,48]{1,2,0:T(8,128)(4,1)S(1)} %broadcast_and_fusion, bf16[32,48,128,1]{2,1,3,0:T(8,128)(2,1)} %bitcast.65, bf16[32,48,7,128]{3,2,1,0:T(8,128)(2,1)S(1)} %reshape.237), kind=kOutput, calls=%fused_computation.6 | convolution fusion | flops 133658112 | bytes 5326848 | tf_op jit(solution)/shard_map/vmap(qkgd,pkd->kgqp)/dot_general | solution.py:35
  130.4 2.1 %fusion.1 = f32[32,7,48]{2,1,0:T(8,128)S(1)} fusion(f32[32,48,48,7]{2,1,3,0:T(8,128)S(1)} %get-tuple-element.17, f32[32,7,48]{2,1,0:T(8,128)S(1)} %get-tuple-element.16, pred[32,48,48]{1,2,0:T(8,128)(4,1)S(1)} %broadcast_and_fusion), kind=kLoop, calls=%fused_computation.5 | loop fusion | flops 2053632 | bytes 2224128 | tf_op jit(solution)/shard_map/vmap()/reduce_sum | solution.py:44
  132.5 0.0 copy-start.5
  132.5 0.0 copy-start.7
  132.5 2.3 %fusion = f32[32,128,7]{1,2,0:T(8,128)S(1)} fusion(f32[32,48]{1,0:T(8,128)S(1)} %get-tuple-element.15, bf16[32,48,128,1]{2,1,3,0:T(8,128)(2,1)S(1)} %bitcast.69, f32[32,7,48]{2,1,0:T(8,128)S(1)} %fusion.1, f32[32,48,48,7]{2,1,3,0:T(8,128)S(1)} %get-tuple-element.17, f32[32,7,48]{2,1,0:T(8,128)S(1)} %get-tuple-element.16, ...), kind=kOutput, calls=%fused_computation.2 | convolution fusion | flops 137424896 | bytes 2738176 | tf_op jit(solution)/shard_map/vmap(kgqp,pkd->qkgd)/dot_general | solution.py:45
  134.9 0.1 fusion.17.context
  135.0 0.1 fusion.14
  135.1 0.1 copy.26
  135.2 0.2 convert_element_type.64
  135.4 0.1 copy.45
  135.5 0.1 select_reduce_fusion
  135.6 0.2 convert_reduce_fusion
  135.8 0.8 copy.29.w_out
  136.6 0.6 fusion.31
  137.2 0.7 compare_select_fusion.live
  137.9 2.0 %copy-done = bf16[1,512,3584]{2,1,0:T(8,128)(2,1)S(1)} copy-done((bf16[1,512,3584]{2,1,0:T(8,128)(2,1)S(1)}, bf16[1,512,3584]{2,1,0:T(8,128)(2,1)}, u32[]{:S(2)}) %copy-start) | copy-done | bytes 3670040
  139.9 42.2 %shard_map.110 = bf16[8,16,512]{2,1,0:T(8,128)(2,1)S(1)} custom-call(bf16[32,896]{1,0:T(8,128)(2,1)S(1)} %fusion.17.context, bf16[8,32,448]{2,1,0:T(8,128)(2,1)S(1)} %bitcast.62, bf16[32,32]{1,0:T(8,128)(2,1)S(1)} %bitcast.63, bf16[896,448]{1,0:T(8,128)(2,1)S(1)} %copy.29.w_out, bf16[512,3584]{1,0:T(8,128)(2,1)S(1)} %bitcast.61, ...), custom_call_target="tpu_custom_call" | custom-call | tf_op jit(solution)/shard_map/pallas_call | solution.py:454
  182.1 0.8 fusion.13
  (26 shorter events, 0.1 us)
Async XLA Ops:
  126.4 6.1 %copy-start.3 = (bf16[1536,128]{1,0:T(8,128)(2,1)S(1)}, bf16[1536,128]{1,0:T(8,128)(2,1)}, u32[]{:S(2)}) copy-start(bf16[1536,128]{1,0:T(8,128)(2,1)} %get-tuple-element.10) | copy-start | bytes 1179652
  132.5 2.4 %copy-start.4 = (s32[32]{0:T(128)S(1)}, s32[32]{0:T(128)}, u32[]{:S(2)}) copy-start(s32[32]{0:T(128)} %param.17) | copy-start | bytes 388
  132.5 2.5 %copy-start.2 = (f32[4,32,896]{2,1,0:T(8,128)S(1)}, f32[4,32,896]{2,1,0:T(8,128)}, u32[]{:S(2)}) copy-start(f32[4,32,896]{2,1,0:T(8,128)} %get-tuple-element.8) | copy-start | bytes 1376260
  132.5 3.0 %copy-start.5 = (s32[8]{0:T(128)S(1)}, s32[8]{0:T(128)}, u32[]{:S(2)}) copy-start(s32[8]{0:T(128)} %param.19) | copy-start | bytes 100
  132.5 3.0 %copy-start.7 = (s32[32,1]{0,1:T(1,128)S(1)}, s32[32,1]{0,1:T(1,128)}, u32[]{:S(2)}) copy-start(s32[32,1]{0,1:T(1,128)} %param.18) | copy-start | bytes 388
  132.5 3.3 %copy-start.1 = (bf16[896,448]{0,1:T(8,128)(2,1)S(1)}, bf16[896,448]{0,1:T(8,128)(2,1)}, u32[]{:S(2)}) copy-start(bf16[896,448]{0,1:T(8,128)(2,1)} %param.15) | copy-start | bytes 2408452
  132.5 4.1 %copy-start.6 = (s32[8]{0:T(128)S(1)}, s32[8]{0:T(128)}, u32[]{:S(2)}) copy-start(s32[8]{0:T(128)} %param.20) | copy-start | bytes 100
  134.8 47.3 %copy-start.8 = (s32[32]{0:T(128)S(1)}, s32[32]{0:T(128)}, u32[]{:S(2)}) copy-start(s32[32]{0:T(128)} %param.21) | copy-start | bytes 388
  137.9 2.0 %copy-start = (bf16[1,512,3584]{2,1,0:T(8,128)(2,1)S(1)}, bf16[1,512,3584]{2,1,0:T(8,128)(2,1)}, u32[]{:S(2)}) copy-start(bf16[1,512,3584]{2,1,0:T(8,128)(2,1)} %param.16) | copy-start | bytes 11010052

commit v3 on v2

--- a/solution.py
+++ b/solution.py
@@ -2,6 +2,7 @@
 
 import jax
 import jax.numpy as jnp
+import numpy as np
 from jax import lax
 from jax.experimental import pallas as pl
 from jax.experimental.pallas import tpu as pltpu
@@ -50,12 +51,13 @@
 
 MESH = pl.DeviceIdType.MESH
 ROWS = 384
+CHUNK = 4
 
 
 def gather_project_kernel(
-    tin, win, gain, mask, cosine, sine, qkv, pooled,
-    tok, wbuf, scaled, acc, squares,
-    tsend, trecv, wsend, wrecv, lsem,
+    tin, query_in, keyval_in, gain, lens, cosine, sine, place, context, pooled,
+    tok, wbuf, scaled, acc, squares, mask, stash, heads,
+    tsend, trecv, wsend, wrecv, hsend, hrecv, lsem,
 ):
     dp = lax.axis_index("dp")
     mp = lax.axis_index("mp")
@@ -65,6 +67,15 @@
     far = (core_peer + 2) % 4
     x_peer = 2 * z + 1 - x
     total = tin.shape[0]
+    depth, columns = wbuf.shape[1:]
+    queries = query_in.shape[1]
+    seq_len = total // lens.shape[0]
+    own_query = pltpu.make_async_copy(query_in, wbuf.at[dp, :, pl.ds(0, queries)], lsem.at[0])
+    own_keyval = pltpu.make_async_copy(
+        keyval_in, wbuf.at[dp, :, pl.ds(queries, columns - queries)], lsem.at[1]
+    )
+    own_query.start()
+    own_keyval.start()
 
     barrier = pltpu.get_barrier_semaphore()
 
@@ -100,11 +111,11 @@
             recv_sem=trecv.at[index], device_id={"dp": dp, "mp": mp_to}, device_id_type=MESH,
         )
 
-    def weight_copy(way, z_from, source):
+    def weight_copy(way, z_from):
         slot = 2 * z_from + x
         dp_to = (dp + 2, dp - 2, x_peer)[way]
         return pltpu.make_async_remote_copy(
-            src_ref=wbuf.at[slot] if source is None else source, dst_ref=wbuf.at[slot],
+            src_ref=wbuf.at[slot], dst_ref=wbuf.at[slot],
             send_sem=wsend.at[way, z_from], recv_sem=wrecv.at[slot],
             device_id={"dp": dp_to, "mp": mp}, device_id_type=MESH,
         )
@@ -115,39 +126,87 @@
             recv_sem=wrecv.at[slot], device_id={"dp": x_peer, "mp": mp}, device_id_type=MESH,
         ).wait_recv()
 
+    pair = z + 1 - 2 * (z % 2)
+    upper, lower = pl.ds(0, depth // 2), pl.ds(depth // 2, depth // 2)
+
+    def pair_upper():
+        slot = 2 * pair + x
+        return pltpu.make_async_remote_copy(
+            src_ref=wbuf.at[slot, upper], dst_ref=wbuf.at[slot, upper],
+            send_sem=hsend.at[0], recv_sem=hrecv.at[0],
+            device_id={"dp": x_peer, "mp": mp}, device_id_type=MESH,
+        )
+
+    def pair_lower():
+        slot = 2 * z + 1 - x
+        return pltpu.make_async_remote_copy(
+            src_ref=wbuf.at[slot, lower], dst_ref=wbuf.at[slot, lower],
+            send_sem=hsend.at[1], recv_sem=hrecv.at[1],
+            device_id={"dp": 2 * pair + x, "mp": mp}, device_id_type=MESH,
+        )
+
+    def pair_arrival(index, rows):
+        slot = 2 * pair + 1 - x
+        pltpu.make_async_remote_copy(
+            src_ref=wbuf.at[slot, rows], dst_ref=wbuf.at[slot, rows],
+            send_sem=hsend.at[index], recv_sem=hrecv.at[index],
+            device_id={"dp": x_peer, "mp": mp}, device_id_type=MESH,
+        ).wait_recv()
+
     across = token_copy(0, tin, mp, y_peer)
     across.start()
+    own_query.wait()
+    own_keyval.wait()
 
     @pl.when(has_up)
     def _():
-        weight_copy(0, z, win).start()
+        weight_copy(0, z).start()
 
     @pl.when(has_down)
     def _():
-        weight_copy(1, z, win).start()
-
-    weight_copy(2, z, win).start()
+        weight_copy(1, z).start()
+
+    weight_copy(2, z).start()
     beside = token_copy(1, tin, mp, core_peer)
     beside.start()
-    own = pltpu.make_async_copy(win, wbuf.at[dp], lsem)
-    own.start()
 
     squares[...] = jnp.zeros_like(squares)
+    index = lax.broadcasted_iota(jnp.int32, mask.shape, 1)
+    first = lax.broadcasted_iota(jnp.int32, mask.shape, 0) * seq_len
+    ahead = (index - first).astype(jnp.float32)
+    mask[...] = jnp.where((ahead >= 0.0) & (ahead < lens[:, 0:1]), 1.0, 0.0).astype(mask.dtype)
 
     def prepare(source, slot):
+        part = tin.shape[1]
+        factor = gain[:, pl.ds(pl.multiple_of(slot * part, 128), part)]
+
         @pl.loop(0, total // 96)
         def _(step):
             rows = pl.ds(pl.multiple_of(step * 96, 96), 96)
             values = source[rows, :].astype(jnp.float32)
             squares[rows, :] += jnp.sum(values * values, axis=-1, keepdims=True)
-            scaled[slot, rows, :] = (values * gain[slot]).astype(jnp.bfloat16)
-
-        pooled[slot] = jnp.dot(mask[...], source[...], preferred_element_type=jnp.float32)
+            scaled[slot, rows, :] = (values * factor).astype(jnp.bfloat16)
+
+        mean = jnp.dot(mask[...], source[...], preferred_element_type=jnp.float32) / lens[:, 0:1]
+        pooled[2 * slot] = mean[:, : part // 2].astype(pooled.dtype)
+        pooled[2 * slot + 1] = mean[:, part // 2 :].astype(pooled.dtype)
 
     prepare(tin, mp)
     beside.wait_recv()
     prepare(tok.at[core_peer], core_peer)
-    own.wait()
+
+    def send_beside(k, z_from):
+        if k > 1:
+            weight_copy(2, z_from).start()
+            return
+
+        @pl.when(z_from == pair)
+        def _():
+            pair_upper().start()
+
+        @pl.when(z_from != pair)
+        def _():
+            weight_copy(2, z_from).start()
 
     def relay(k):
         @pl.when(z >= k)
@@ -156,9 +215,9 @@
 
             @pl.when(has_up)
             def _():
-                weight_copy(0, z - k, None).start()
-
-            weight_copy(2, z - k, None).start()
+                weight_copy(0, z - k).start()
+
+            send_beside(k, z - k)
 
         @pl.when(z + k <= 3)
         def _():
@@ -166,11 +225,13 @@
 
             @pl.when(has_down)
             def _():
-                weight_copy(1, z + k, None).start()
-
-            weight_copy(2, z + k, None).start()
+                weight_copy(1, z + k).start()
+
+            send_beside(k, z + k)
 
     relay(1)
+    weight_arrival(2 * z + 1 - x)
+    pair_lower().start()
     relay(2)
     across.wait_recv()
     onward = token_copy(2, tok.at[y_peer], y_peer, core_peer)
@@ -181,11 +242,14 @@
     prepare(tok.at[far], far)
 
     width = 4 * tin.shape[1]
-    columns = win.shape[1]
 
     def multiply(turn):
-        block = (z, z + 1 - 2 * (z % 2), (z + 2) % 4, 3 - z)[turn]
-        weight_arrival(2 * block + 1 - x)
+        block = (z, pair, (z + 2) % 4, 3 - z)[turn]
+        if turn == 1:
+            pair_arrival(0, upper)
+            pair_arrival(1, lower)
+        elif turn > 1:
+            weight_arrival(2 * block + 1 - x)
         weights = wbuf.at[pl.ds(2 * block, 2)]
 
         @pl.loop(0, total // ROWS)
@@ -193,7 +257,7 @@
             rows = pl.ds(pl.multiple_of(step * ROWS, ROWS), ROWS)
             product = jnp.dot(
                 scaled[block, rows, :],
-                weights[...].reshape(2 * win.shape[0], columns),
+                weights[...].reshape(2 * depth, columns),
                 preferred_element_type=jnp.float32,
             )
             if turn == 0:
@@ -204,16 +268,52 @@
     for turn in range(4):
         multiply(turn)
 
-    @pl.loop(0, total // ROWS)
+    group = queries // HEAD_DIM
+    lanes = (group + 1) * seq_len
+    key_pos = lax.broadcasted_iota(jnp.int32, (seq_len, lanes), 0).astype(jnp.float32)
+    query_pos = place[...]
+    causal = key_pos <= query_pos
+    head_start = lax.broadcasted_iota(jnp.int32, (8, lanes), 0) * seq_len
+    offset = lax.broadcasted_iota(jnp.int32, (8, lanes), 1) - head_start
+    same_head = (offset >= 0) & (offset < seq_len)
+    block_rows = CHUNK * seq_len
+
+    @pl.loop(0, total // block_rows)
     def _(step):
-        rows = pl.ds(pl.multiple_of(step * ROWS, ROWS), ROWS)
+        rows = pl.ds(pl.multiple_of(step * block_rows, block_rows), block_rows)
         scale = lax.rsqrt(squares[rows, :] * (1.0 / width) + 1e-06)
         for head in range(columns // HEAD_DIM):
             span = pl.ds(head * HEAD_DIM, HEAD_DIM)
             piece = acc[rows, span] * scale
             if head < columns // HEAD_DIM - 1:
                 piece = piece * cosine[...] + pltpu.roll(piece, HEAD_DIM // 2, 1) * sine[...]
-            qkv[rows, span] = piece.astype(jnp.bfloat16)
+            stash[:, span] = piece.astype(jnp.bfloat16)
+        for item in range(CHUNK):
+            here = slice(item * seq_len, (item + 1) * seq_len)
+            stacked = jnp.concatenate(
+                [stash[here, h * HEAD_DIM : (h + 1) * HEAD_DIM] for h in range(group + 1)], axis=0
+            )
+            keys = stash[here, queries : queries + HEAD_DIM]
+            values = stash[here, queries + HEAD_DIM :]
+            length = lens[pl.ds(step * CHUNK + item, 1), 0:1]
+            scores = lax.dot_general(
+                keys, stacked, (((1,), (1,)), ((), ())), preferred_element_type=jnp.float32
+            ) * (1.0 / math.sqrt(HEAD_DIM))
+            scores = jnp.where(causal & (key_pos < length), scores, -1e30)
+            expanded = jnp.exp(scores - jnp.max(scores, axis=0, keepdims=True))
+            weights = (expanded / jnp.sum(expanded, axis=0, keepdims=True)).astype(jnp.bfloat16)
+            chosen = jnp.where(same_head & (query_pos < length), 1.0, 0.0).astype(jnp.bfloat16)
+            sums = lax.dot_general(
+                chosen, weights, (((1,), (1,)), ((), ())), preferred_element_type=jnp.float32
+            )
+            high = sums.astype(jnp.bfloat16).astype(jnp.float32)
+            both = jnp.concatenate([high, sums - high], axis=0).astype(jnp.bfloat16)
+            mixed = jnp.dot(both, values, preferred_element_type=jnp.float32)
+            result = (mixed[:8] + mixed[8:]) / length
+            heads[step * CHUNK + item] = result
+
+    for h in range(group):
+        context[:, h * HEAD_DIM : (h + 1) * HEAD_DIM] = heads[:, h, :]
 
     across.wait_send()
     beside.wait_send()
@@ -222,39 +322,42 @@
     for z_from in range(4):
         @pl.when(has_up & (z >= z_from))
         def _():
-            weight_copy(0, z_from, None).wait_send()
+            weight_copy(0, z_from).wait_send()
 
         @pl.when(has_down & (z <= z_from))
         def _():
-            weight_copy(1, z_from, None).wait_send()
-
-        weight_copy(2, z_from, None).wait_send()
+            weight_copy(1, z_from).wait_send()
+
+        @pl.when(z_from != pair)
+        def _():
+            weight_copy(2, z_from).wait_send()
+
+    pair_upper().wait_send()
+    pair_lower().wait_send()
 
 
 def gather_project(tokens, norm_gain, w_query, w_keyval, lengths):
     dialogs, seq_len, part = tokens.shape
     total = dialogs * seq_len
-    weights = jnp.concatenate([w_query, w_keyval.reshape(w_keyval.shape[0], -1)], axis=1)
-    depth, columns = weights.shape
-    positions = jnp.arange(seq_len)
+    depth, queries = w_query.shape
+    keyval = w_keyval.reshape(depth, -1)
+    columns = queries + keyval.shape[1]
     half = HEAD_DIM // 2
-    freqs = rope_base ** (-jnp.arange(half, dtype=jnp.float32) * 2.0 / HEAD_DIM)
-    angles = positions.astype(jnp.float32)[:, None] * freqs[None, :]
-    cosine = jnp.cos(angles)
-    sine = jnp.sin(angles)
-    cosine = jnp.tile(jnp.concatenate([cosine, cosine], axis=1), (ROWS // seq_len, 1))
-    sine = jnp.tile(jnp.concatenate([-sine, sine], axis=1), (ROWS // seq_len, 1))
-    row = jnp.arange(total)[None, :]
-    mine = jnp.arange(dialogs)[:, None]
-    mask = ((row // seq_len == mine) & (row % seq_len < lengths[:, None])).astype(jnp.bfloat16)
+    freqs = rope_base ** (-np.arange(half, dtype=np.float64) * 2.0 / HEAD_DIM)
+    angles = np.arange(seq_len, dtype=np.float64)[:, None] * freqs[None, :]
+    cosine, sine = np.cos(angles), np.sin(angles)
+    cosine = np.tile(np.concatenate([cosine, cosine], axis=1), (CHUNK, 1)).astype(np.float32)
+    sine = np.tile(np.concatenate([-sine, sine], axis=1), (CHUNK, 1)).astype(np.float32)
+    place = np.tile(np.arange(seq_len), queries // HEAD_DIM + 1).astype(np.float32)[None, :]
+    lens = jnp.broadcast_to(lengths.astype(jnp.float32)[:, None], (dialogs, 128))
     vmem = pl.BlockSpec(memory_space=pltpu.VMEM)
-    qkv, pooled = pl.pallas_call(
+    return pl.pallas_call(
         gather_project_kernel,
         out_shape=(
-            jax.ShapeDtypeStruct((total, columns), jnp.bfloat16),
-            jax.ShapeDtypeStruct((4, dialogs, part), jnp.float32),
+            jax.ShapeDtypeStruct((dialogs, queries), jnp.float32),
+            jax.ShapeDtypeStruct((8, dialogs, part // 2), jnp.bfloat16),
         ),
-        in_specs=[vmem] * 6,
+        in_specs=[vmem] * 8,
         out_specs=(vmem, vmem),
         scratch_shapes=[
             pltpu.VMEM((4, total, part), jnp.bfloat16),
@@ -262,37 +365,36 @@
             pltpu.VMEM((4, total, part), jnp.bfloat16),
             pltpu.VMEM((total, columns), jnp.float32),
             pltpu.VMEM((total, 1), jnp.float32),
+            pltpu.VMEM((dialogs, total), jnp.bfloat16),
+            pltpu.VMEM((CHUNK * seq_len, columns), jnp.bfloat16),
+            pltpu.VMEM((dialogs, 8, HEAD_DIM), jnp.float32),
             pltpu.SemaphoreType.DMA((3,)),
             pltpu.SemaphoreType.DMA((3,)),
             pltpu.SemaphoreType.DMA((3, 4)),
             pltpu.SemaphoreType.DMA((8,)),
-            pltpu.SemaphoreType.DMA,
+            pltpu.SemaphoreType.DMA((2,)),
+            pltpu.SemaphoreType.DMA((2,)),
+            pltpu.SemaphoreType.DMA((2,)),
         ],
         compiler_params=pltpu.CompilerParams(
             collective_id=0, has_side_effects=True, vmem_limit_bytes=58 * 1024 * 1024
         ),
     )(
-        tokens.reshape(total, part), weights, norm_gain.reshape(4, 1, part), mask, cosine, sine
-    )
-    pooled_input = (pooled / lengths.astype(jnp.float32)[None, :, None]).transpose(1, 0, 2)
-    queries = w_query.shape[1]
-    shape = (dialogs, seq_len, -1, HEAD_DIM)
-    return (
-        qkv[:, :queries].reshape(shape),
-        qkv[:, queries : queries + HEAD_DIM].reshape(shape),
-        qkv[:, queries + HEAD_DIM :].reshape(shape),
-        pooled_input.reshape(dialogs, 4 * part),
+        tokens.reshape(total, part), w_query, keyval, norm_gain.reshape(1, -1), lens, cosine, sine,
+        place,
     )
 
 
 def score_kernel(
-    context, pooled, onehot, w_out, members, live, returned,
+    context, pooled, onehot, w_out, members_in, live, returned, members,
     own_rows, own_pooled, all_rows, all_pooled, exact, parts, others, sums, rows_in, joined,
     squares, replies, arrived,
-    a_send, a_recv, c_send, c_recv, d_send, d_recv, f_send, f_recv,
+    a_send, a_recv, c_send, c_recv, d_send, d_recv, f_send, f_recv, l_sem,
 ):
     dp = lax.axis_index("dp")
     mp = lax.axis_index("mp")
+    load = pltpu.make_async_copy(members_in, members, l_sem)
+    load.start()
     barrier = pltpu.get_barrier_semaphore()
     for i in range(8):
         for j in range(4):
@@ -307,7 +409,7 @@
             onehot[...], pooled[o], preferred_element_type=jnp.float32
         ).astype(jnp.bfloat16)
     own_rows[...] = jnp.dot(
-        onehot[...], context[...], preferred_element_type=jnp.float32
+        onehot[...], context[...].astype(jnp.bfloat16), preferred_element_type=jnp.float32
     ).astype(jnp.bfloat16)
     pl.semaphore_wait(barrier, 31)
 
@@ -334,6 +436,8 @@
         pooled_copy(i, dp).start()
     all_rows[dp] = own_rows[...]
     all_pooled[dp] = own_pooled[dp]
+
+    load.wait()
 
     @pl.loop(0, members.shape[0] // 64)
     def _(step):
@@ -448,15 +552,15 @@
     width = w_out.shape[1]
     member_count = members.shape[0]
     slots = onehot.reshape(-1, dialogs).astype(jnp.bfloat16)
-    pooled = pooled_input.astype(jnp.bfloat16).reshape(dialogs, 8, width).transpose(1, 0, 2)
     vmem = pl.BlockSpec(memory_space=pltpu.VMEM)
     half, full = jnp.bfloat16, jnp.float32
     returned = pl.pallas_call(
         score_kernel,
         out_shape=jax.ShapeDtypeStruct((8, 16, member_count), half),
-        in_specs=[vmem] * 6,
+        in_specs=[vmem] * 4 + [pl.BlockSpec(memory_space=pl.ANY), vmem],
         out_specs=vmem,
         scratch_shapes=[
+            pltpu.VMEM(members.shape, half),
             pltpu.VMEM((32, head_width), half),
             pltpu.VMEM((8, 32, width), half),
             pltpu.VMEM((8, 32, head_width), half),
@@ -478,11 +582,12 @@
             pltpu.SemaphoreType.DMA((8,)),
             pltpu.SemaphoreType.DMA((8,)),
             pltpu.SemaphoreType.DMA((8,)),
+            pltpu.SemaphoreType.DMA,
         ],
         compiler_params=pltpu.CompilerParams(
             collective_id=1, has_side_effects=True, vmem_limit_bytes=32 * 1024 * 1024
         ),
-    )(pooled_context, pooled, slots, w_out, members, live)
+    )(pooled_context, pooled_input, slots, w_out, members, live)
     return returned[:, : onehot.shape[1]]
 
 
@@ -521,7 +626,8 @@
     pooled_input = (
         jnp.sum(hidden * valid[:, :, None], axis=1) / lengths.astype(jnp.float32)[:, None]
     )
-    return query, keys, values, pooled_input
+    pooled_context = jax.vmap(attend)(query, keys, values, lengths).astype(jnp.bfloat16)
+    return pooled_context, pooled_input
 
 
 def plain_score(pooled_context, pooled_input, w_out, members, onehot, live):
@@ -565,9 +671,8 @@
         project = gather_project
     else:
         project = plain_project
-    query, keys, values, pooled_input = project(tokens, norm_gain, w_query, w_keyval, lengths)
-    dialogs = query.shape[0]
-    pooled_context = jax.vmap(attend)(query, keys, values, lengths).astype(jnp.bfloat16)
+    pooled_context, pooled_input = project(tokens, norm_gain, w_query, w_keyval, lengths)
+    dialogs = tokens.shape[0]
     my_index = lax.axis_index("dp")
     owner_count = lax.axis_size("dp")
     my_count = jnp.sum(jnp.where(owner == my_index, counts, 0))
@@ -606,9 +711,9 @@
         P("dp", "mp"),
         P("dp", None, "mp"),
         P("mp", "dp"),
-        P("dp", "mp", None),
+        P("dp", "mp"),
         P("dp"),
-        P("dp", None),
+        P("dp"),
         P(),
         P(),
         P("dp"),

time: 183 us -> 183 us (level)
  Pallas kernels: 149 us -> 169 us
  local copies, waits for them, and re-layouts: 17.9 us -> 8.31 us
  matrix products: 7.09 us -> 0.82 us
  other arithmetic: 8.73 us -> 3.66 us
    pallas_call x1, Pallas kernels: 107 us -> 128 us  [gather_project(): pl.pallas_call(gather_project_kernel, out_shape=(jax.ShapeDtypeStruct((di...]
    another operation x3 -> x0, local copies, waits for them, and re-layouts: 6.76 us -> none
    dot_general x2 -> x0, matrix products: 6.26 us -> none  [the longest x1 3.98 us: attend(): jnp.einsum('qkgd,pkd->kgqp', grouped, keys, preferred_element_type=jnp.fl...]
    slice x2 -> x0, local copies, waits for them, and re-layouts: 5.62 us -> none  [the longest x1 3.56 us: gather_project(): qkv[:, :queries].reshape(shape)]
    unnamed x20 -> x12, local copies, waits for them, and re-layouts: 3.8 us -> 6.3 us
    concatenate x2 -> x0, other arithmetic: 2.28 us -> none  [the longest x1 2.2 us: gather_project(): jnp.concatenate([w_query, w_keyval.reshape(w_keyval.shape[0], -1)], axis=1)]
    reduce_sum x1 -> x0, other arithmetic: 2.08 us -> none  [attend(): jnp.sum(expanded, axis=-1, keepdims=True)]
where the time goes in v3:
time: 183 us; the launch traced here: 182 us
  Pallas kernels  169 us (92%)
  local copies, waits for them, and re-layouts  8.31 us (5%)
  other arithmetic  3.66 us (2%)
    pallas_call x1, Pallas kernels, gather_project(): pl.pallas_call(gather_project_kernel, out_shape=(jax.ShapeDtypeStruct((di...  128 us
    pallas_call x1, Pallas kernels, score(): pl.pallas_call(score_kernel, out_shape=jax.ShapeDtypeStruct((8, 16, membe...  41.4 us
    unnamed x12, local copies, waits for them, and re-layouts  6.3 us

profile of v3, /device:TPU:0, one launch (start us, length us, event | category | flops | bytes accessed | tf_op | source)
XLA Modules:
  0.0 182.3 jit_solution(16684600794475831173)
XLA Ops:
  0.0 0.0 copy-start.3
  0.0 0.8 select_reduce_fusion
  0.8 0.2 convert_reduce_fusion
  1.1 1.3 fusion.6
  2.4 0.7 compare_select_fusion.live
  3.0 1.7 copy.25
  4.7 0.7 convert_element_type.16
  5.3 0.7 broadcast_in_dim.28.lens
  6.0 1.3 reshape.81.gain
  7.3 128.0 %shard_map.136 = (f32[32,896]{1,0:T(8,128)}, bf16[8,32,448]{2,1,0:T(8,128)(2,1)}) custom-call(bf16[1536,896]{1,0:T(8,128)(2,1)} %bitcast.14, bf16[448,896]{1,0:T(8,128)(2,1)} %query_in.1, bf16[448,256]{1,0:T(8,128)(2,1)} %bitcast.15, f32[1,3584]{1,0:T(1,128)} %reshape.81.gain, f32[32,128]{1,0:T(8,128)} %broadcast_in_dim.28.lens, ...), custom_call_target="tpu_custom_call" | custom-call | tf_op jit(solution)/shard_map/pallas_call | solution.py:354
  135.4 0.0 copy-start.4
  135.4 0.0 copy-done.3
  135.4 0.8 copy.19.w_out
  136.2 0.0 copy-start
  136.2 2.0 %copy-done = bf16[1,512,3584]{2,1,0:T(8,128)(2,1)S(1)} copy-done((bf16[1,512,3584]{2,1,0:T(8,128)(2,1)S(1)}, bf16[1,512,3584]{2,1,0:T(8,128)(2,1)}, u32[]{:S(2)}) %copy-start) | copy-done | bytes 3670040
  138.2 0.0 copy-start.1
  138.2 0.9 copy-done.1
  139.2 0.0 copy-start.2
  139.2 0.9 copy-done.2
  140.1 41.4 %shard_map.137 = bf16[8,16,512]{2,1,0:T(8,128)(2,1)S(1)} custom-call(f32[32,896]{1,0:T(8,128)S(1)} %copy-done.2, bf16[8,32,448]{2,1,0:T(8,128)(2,1)S(1)} %copy-done.1, bf16[32,32]{1,0:T(8,128)(2,1)S(1)} %bitcast.13, bf16[896,448]{1,0:T(8,128)(2,1)S(1)} %copy.19.w_out, bf16[512,3584]{1,0:T(8,128)(2,1)S(1)} %bitcast.12, f32[1,512]{1,0:T(1,128)S(1)} %compare_select_fusion.live), custom_call_target="tpu_custom_call" | custom-call | tf_op jit(solution)/shard_map/pallas_call | solution.py:557
  181.5 0.0 copy-done.4
  181.5 0.8 fusion
  (6 shorter events, 0.1 us)
Async XLA Ops:
  0.0 135.4 %copy-start.3 = (bf16[896,448]{0,1:T(8,128)(2,1)S(1)}, bf16[896,448]{0,1:T(8,128)(2,1)}, u32[]{:S(2)}) copy-start(bf16[896,448]{0,1:T(8,128)(2,1)} %param.18) | copy-start | bytes 2408452
  135.4 46.1 %copy-start.4 = (s32[32]{0:T(128)S(1)}, s32[32]{0:T(128)}, u32[]{:S(2)}) copy-start(s32[32]{0:T(128)} %param.24) | copy-start | bytes 388
  136.2 2.0 %copy-start = (bf16[1,512,3584]{2,1,0:T(8,128)(2,1)S(1)}, bf16[1,512,3584]{2,1,0:T(8,128)(2,1)}, u32[]{:S(2)}) copy-start(bf16[1,512,3584]{2,1,0:T(8,128)(2,1)} %param.19) | copy-start | bytes 11010052
  138.2 0.9 copy-start.1
  139.2 0.9 copy-start.2

commit v4 on v3

--- a/solution.py
+++ b/solution.py
@@ -57,7 +57,7 @@
 def gather_project_kernel(
     tin, query_in, keyval_in, gain, lens, cosine, sine, place, context, pooled,
     tok, wbuf, scaled, acc, squares, mask, stash, heads,
-    tsend, trecv, wsend, wrecv, hsend, hrecv, lsem,
+    tsend, trecv, wsend, wrecv, lsem,
 ):
     dp = lax.axis_index("dp")
     mp = lax.axis_index("mp")
@@ -127,31 +127,6 @@
         ).wait_recv()
 
     pair = z + 1 - 2 * (z % 2)
-    upper, lower = pl.ds(0, depth // 2), pl.ds(depth // 2, depth // 2)
-
-    def pair_upper():
-        slot = 2 * pair + x
-        return pltpu.make_async_remote_copy(
-            src_ref=wbuf.at[slot, upper], dst_ref=wbuf.at[slot, upper],
-            send_sem=hsend.at[0], recv_sem=hrecv.at[0],
-            device_id={"dp": x_peer, "mp": mp}, device_id_type=MESH,
-        )
-
-    def pair_lower():
-        slot = 2 * z + 1 - x
-        return pltpu.make_async_remote_copy(
-            src_ref=wbuf.at[slot, lower], dst_ref=wbuf.at[slot, lower],
-            send_sem=hsend.at[1], recv_sem=hrecv.at[1],
-            device_id={"dp": 2 * pair + x, "mp": mp}, device_id_type=MESH,
-        )
-
-    def pair_arrival(index, rows):
-        slot = 2 * pair + 1 - x
-        pltpu.make_async_remote_copy(
-            src_ref=wbuf.at[slot, rows], dst_ref=wbuf.at[slot, rows],
-            send_sem=hsend.at[index], recv_sem=hrecv.at[index],
-            device_id={"dp": x_peer, "mp": mp}, device_id_type=MESH,
-        ).wait_recv()
 
     across = token_copy(0, tin, mp, y_peer)
     across.start()
@@ -195,19 +170,6 @@
     beside.wait_recv()
     prepare(tok.at[core_peer], core_peer)
 
-    def send_beside(k, z_from):
-        if k > 1:
-            weight_copy(2, z_from).start()
-            return
-
-        @pl.when(z_from == pair)
-        def _():
-            pair_upper().start()
-
-        @pl.when(z_from != pair)
-        def _():
-            weight_copy(2, z_from).start()
-
     def relay(k):
         @pl.when(z >= k)
         def _():
@@ -217,7 +179,7 @@
             def _():
                 weight_copy(0, z - k).start()
 
-            send_beside(k, z - k)
+            weight_copy(2, z - k).start()
 
         @pl.when(z + k <= 3)
         def _():
@@ -227,11 +189,9 @@
             def _():
                 weight_copy(1, z + k).start()
 
-            send_beside(k, z + k)
+            weight_copy(2, z + k).start()
 
     relay(1)
-    weight_arrival(2 * z + 1 - x)
-    pair_lower().start()
     relay(2)
     across.wait_recv()
     onward = token_copy(2, tok.at[y_peer], y_peer, core_peer)
@@ -245,11 +205,7 @@
 
     def multiply(turn):
         block = (z, pair, (z + 2) % 4, 3 - z)[turn]
-        if turn == 1:
-            pair_arrival(0, upper)
-            pair_arrival(1, lower)
-        elif turn > 1:
-            weight_arrival(2 * block + 1 - x)
+        weight_arrival(2 * block + 1 - x)
         weights = wbuf.at[pl.ds(2 * block, 2)]
 
         @pl.loop(0, total // ROWS)
@@ -328,12 +284,7 @@
         def _():
             weight_copy(1, z_from).wait_send()
 
-        @pl.when(z_from != pair)
-        def _():
-            weight_copy(2, z_from).wait_send()
-
-    pair_upper().wait_send()
-    pair_lower().wait_send()
+        weight_copy(2, z_from).wait_send()
 
 
 def gather_project(tokens, norm_gain, w_query, w_keyval, lengths):
@@ -373,8 +324,6 @@
             pltpu.SemaphoreType.DMA((3, 4)),
             pltpu.SemaphoreType.DMA((8,)),
             pltpu.SemaphoreType.DMA((2,)),
-            pltpu.SemaphoreType.DMA((2,)),
-            pltpu.SemaphoreType.DMA((2,)),
         ],
         compiler_params=pltpu.CompilerParams(
             collective_id=0, has_side_effects=True, vmem_limit_bytes=58 * 1024 * 1024
@@ -557,7 +506,7 @@
     returned = pl.pallas_call(
         score_kernel,
         out_shape=jax.ShapeDtypeStruct((8, 16, member_count), half),
-        in_specs=[vmem] * 4 + [pl.BlockSpec(memory_space=pl.ANY), vmem],
+        in_specs=[vmem] * 4 + [pl.BlockSpec(memory_space=pltpu.HBM), vmem],
         out_specs=vmem,
         scratch_shapes=[
             pltpu.VMEM(members.shape, half),

time: 183 us -> 173 us (0.945)
  Pallas kernels: 169 us -> 159 us
    pallas_call x1, Pallas kernels: 128 us -> 117 us  [gather_project(): pl.pallas_call(gather_project_kernel, out_shape=(jax.ShapeDtypeStruct((di...]
where the time goes in v4:
time: 173 us; the launch traced here: 172 us
  Pallas kernels  159 us (92%)
  local copies, waits for them, and re-layouts  8.31 us (5%)
  other arithmetic  3.66 us (2%)
    pallas_call x1, Pallas kernels, gather_project(): pl.pallas_call(gather_project_kernel, out_shape=(jax.ShapeDtypeStruct((di...  117 us
    pallas_call x1, Pallas kernels, score(): pl.pallas_call(score_kernel, out_shape=jax.ShapeDtypeStruct((8, 16, membe...  42.5 us
    unnamed x12, local copies, waits for them, and re-layouts  6.3 us

profile of v4, /device:TPU:0, one launch (start us, length us, event | category | flops | bytes accessed | tf_op | source)
XLA Modules:
  0.0 172.4 jit_solution(6161274661200592644)
XLA Ops:
  0.0 0.0 copy-start.3
  0.0 0.8 select_reduce_fusion
  0.8 0.2 convert_reduce_fusion
  1.1 1.3 fusion.6
  2.4 0.7 compare_select_fusion.live
  3.0 1.7 copy.25
  4.7 0.7 convert_element_type.16
  5.3 0.7 broadcast_in_dim.28.lens
  6.0 1.3 reshape.81.gain
  7.3 117.0 %shard_map.136 = (f32[32,896]{1,0:T(8,128)}, bf16[8,32,448]{2,1,0:T(8,128)(2,1)}) custom-call(bf16[1536,896]{1,0:T(8,128)(2,1)} %bitcast.14, bf16[448,896]{1,0:T(8,128)(2,1)} %query_in.1, bf16[448,256]{1,0:T(8,128)(2,1)} %bitcast.15, f32[1,3584]{1,0:T(1,128)} %reshape.81.gain, f32[32,128]{1,0:T(8,128)} %broadcast_in_dim.28.lens, ...), custom_call_target="tpu_custom_call" | custom-call | tf_op jit(solution)/shard_map/pallas_call | solution.py:305
  124.3 0.0 copy-start.4
  124.3 0.0 copy-done.3
  124.3 0.8 copy.19.w_out
  125.1 0.0 copy-start
  125.1 2.0 %copy-done = bf16[1,512,3584]{2,1,0:T(8,128)(2,1)S(1)} copy-done((bf16[1,512,3584]{2,1,0:T(8,128)(2,1)S(1)}, bf16[1,512,3584]{2,1,0:T(8,128)(2,1)}, u32[]{:S(2)}) %copy-start) | copy-done | bytes 3670040
  127.1 0.0 copy-start.1
  127.1 0.9 copy-done.1
  128.1 0.0 copy-start.2
  128.1 0.9 copy-done.2
  129.0 42.5 %shard_map.137 = bf16[8,16,512]{2,1,0:T(8,128)(2,1)S(1)} custom-call(f32[32,896]{1,0:T(8,128)S(1)} %copy-done.2, bf16[8,32,448]{2,1,0:T(8,128)(2,1)S(1)} %copy-done.1, bf16[32,32]{1,0:T(8,128)(2,1)S(1)} %bitcast.13, bf16[896,448]{1,0:T(8,128)(2,1)S(1)} %copy.19.w_out, bf16[512,3584]{1,0:T(8,128)(2,1)S(1)} %bitcast.12, f32[1,512]{1,0:T(1,128)S(1)} %compare_select_fusion.live), custom_call_target="tpu_custom_call" | custom-call | tf_op jit(solution)/shard_map/pallas_call | solution.py:506
  171.5 0.0 copy-done.4
  171.5 0.8 fusion
  (6 shorter events, 0.1 us)
Async XLA Ops:
  0.0 124.3 %copy-start.3 = (bf16[896,448]{0,1:T(8,128)(2,1)S(1)}, bf16[896,448]{0,1:T(8,128)(2,1)}, u32[]{:S(2)}) copy-start(bf16[896,448]{0,1:T(8,128)(2,1)} %param.18) | copy-start | bytes 2408452
  124.3 47.2 %copy-start.4 = (s32[32]{0:T(128)S(1)}, s32[32]{0:T(128)}, u32[]{:S(2)}) copy-start(s32[32]{0:T(128)} %param.24) | copy-start | bytes 388
  125.1 2.0 %copy-start = (bf16[1,512,3584]{2,1,0:T(8,128)(2,1)S(1)}, bf16[1,512,3584]{2,1,0:T(8,128)(2,1)}, u32[]{:S(2)}) copy-start(bf16[1,512,3584]{2,1,0:T(8,128)(2,1)} %param.19) | copy-start | bytes 11010052
  127.1 0.9 copy-start.1
  128.1 0.9 copy-start.2
